TPU v7x, 256 devices: a whole 4x4x8 slice. The times are simulated.
256 devices in a mesh: ctx: 32 (over z_lo, y, x), head: 8 (over z_hi, core).
Axes of the slice: x: 4, y: 4, z: 8 (z_hi: 4, z_lo: 2; z = z_hi * 2 + z_lo), core: 2. Of those that a mesh axis runs over, the one named last changes fastest.
Arguments:
- queries: bfloat16 [8192, 5120], P('ctx', 'head'), may hold values from -800 to 800
- keys: bfloat16 [8192, 5120], P('ctx', 'head'), may hold values from -800 to 800
- values: bfloat16 [8192, 5120], P('ctx', 'head'), may hold values from -6 to 6
- q_gain: float32 [5120], P('head'), may hold values from 0.6 to 1.5
- k_gain: float32 [5120], P('head'), may hold values from 0.6 to 1.5
- ref_keys: bfloat16 [32768, 5120], P('ctx', 'head'), may hold values from -6 to 6
- ref_values: bfloat16 [32768, 5120], P('ctx', 'head'), may hold values from -6 to 6
- out_weight: bfloat16 [5120, 5120], P('head'), may hold values from -0.078125 to 0.078125
- partners: int32 [32, 2, 12], replicated, may hold values from 0 to 63, as said below
- owners: int32 [2], replicated, may hold values from 0 to 31, as said below
- labels: int32 [64], P('ctx'), may hold values from 0 to 1
Outputs:
- attended: bfloat16 [8192, 5120], P('ctx', 'head')
- mixed: bfloat16 [8192, 5120], P('ctx', 'head')
Inputs may be any that keep to these rules, and one draw needn't show every extreme that they name: `partners`: over both persons' lists of one context shard, the blocks of any one shard are named at most 1 times, and the blocks of some shard exactly 1 times. `owners`: the persons' identity shards differ, and one of them is the last shard.
All inputs are finite; a program needn't handle non-finite values.
Results may differ from a plain program's by a relative error of at most 0.018.
Values may be sent and summed in bfloat16 or wider, within the bound.
A program may use at most 128 MiB of HBM per device.

v0:
```python
import jax
import jax.numpy as jnp
from jax import lax
from jax.sharding import PartitionSpec as P

D = 5120
HD = 128
BLK = 128


epsilon = 1e-06


def spread(value, axis, source):
    kept = jnp.where(lax.axis_index(axis) == source, value, 0).astype(value.dtype)
    return lax.psum(kept, axis)


def normalize(features, scale_gain, square_total):
    factor = lax.rsqrt(square_total / D + epsilon)
    return (features * factor[:, None] * scale_gain[None, :]).astype(jnp.bfloat16)


def attend_block(query, own_keys, own_values, far_keys, far_values, bank_keys, bank_values):
    row_count, width = query.shape
    head_count = width // HD
    key_set = jnp.concatenate([own_keys, far_keys, bank_keys], axis=0)
    value_set = jnp.concatenate([own_values, far_values, bank_values], axis=0)
    query_heads = query.reshape(row_count, head_count, HD)
    key_heads = key_set.reshape(-1, head_count, HD)
    value_heads = value_set.reshape(-1, head_count, HD)
    scores = jnp.einsum(
        "qhd,khd->hqk", query_heads, key_heads, preferred_element_type=jnp.float32
    ) * HD ** (-0.5)
    row_peak = jnp.max(scores, axis=2, keepdims=True)
    exponent = jnp.exp(scores - row_peak)
    denominator = jnp.sum(exponent, axis=2)
    weights = exponent.astype(jnp.bfloat16)
    combined = jnp.einsum("hqk,khd->qhd", weights, value_heads, preferred_element_type=jnp.float32)
    return (combined / denominator.T[:, :, None]).reshape(row_count, width).astype(jnp.bfloat16)


def shards(
    queries,
    keys,
    values,
    q_gain,
    k_gain,
    ref_keys,
    ref_values,
    out_weight,
    partners,
    owners,
    labels,
):
    tokens, width = queries.shape
    blocks = tokens // BLK
    own_index = lax.axis_index("ctx")
    persons = partners.shape[1]
    q_float = queries.astype(jnp.float32)
    k_float = keys.astype(jnp.float32)
    q_total, k_total = lax.psum(
        (jnp.sum(q_float * q_float, axis=1), jnp.sum(k_float * k_float, axis=1)), "head"
    )
    q_norm = normalize(q_float, q_gain, q_total)
    k_norm = normalize(k_float, k_gain, k_total)
    query_blocks = q_norm.reshape(blocks, BLK, width)
    key_blocks = k_norm.reshape(blocks, BLK, width)
    value_blocks = values.reshape(blocks, BLK, width)
    wanted = partners[own_index].reshape(-1)
    whole_keys, whole_values = (
        lax.all_gather(k_norm, "ctx", axis=0, tiled=True),
        lax.all_gather(values, "ctx", axis=0, tiled=True),
    )
    far_keys = whole_keys.reshape(-1, BLK, width)[wanted]
    far_values = whole_values.reshape(-1, BLK, width)[wanted]
    far_keys = far_keys.reshape(persons, -1, width)
    far_values = far_values.reshape(persons, -1, width)
    local_bank = jnp.stack([ref_keys, ref_values])
    identities = []
    for person in range(persons):
        identities.append(spread(local_bank, "ctx", owners[person]))
    identity_stack = jnp.stack(identities)

    def one_block(position):
        person_label = labels[position]
        return attend_block(
            query_blocks[position],
            key_blocks[position],
            value_blocks[position],
            far_keys[person_label],
            far_values[person_label],
            identity_stack[person_label, 0],
            identity_stack[person_label, 1],
        )

    attended = lax.map(one_block, jnp.arange(blocks)).reshape(tokens, width)
    partial_out = jnp.dot(attended, out_weight, preferred_element_type=jnp.float32)
    mixed = lax.psum_scatter(
        partial_out.astype(jnp.bfloat16), "head", scatter_dimension=1, tiled=True
    )
    return (attended, mixed)


def solution(mesh):
    return jax.shard_map(
        shards,
        mesh=mesh,
        in_specs=(
            P("ctx", "head"),
            P("ctx", "head"),
            P("ctx", "head"),
            P("head"),
            P("head"),
            P("ctx", "head"),
            P("ctx", "head"),
            P("head", None),
            P(),
            P(),
            P("ctx"),
        ),
        out_specs=(P("ctx", "head"), P("ctx", "head")),
        check_vma=False,
    )
```

profile of v0, /device:TPU:2, one launch (start us, length us, event | category | flops | bytes accessed | tf_op | source)
XLA Modules:
  0.0 848.1 jit_solution(13434496772358359575)
XLA Ops:
  9.8 1.6 copy.45
  11.5 1.6 copy.46
  13.1 2.8 select_bitcast_fusion.1
  17.1 19.9 %all-reduce = (f32[256]{0:T(256)S(1)}, f32[256]{0:T(256)S(1)}) all-reduce(f32[256]{0:T(256)S(1)} %get-tuple-element.121, f32[256]{0:T(256)S(1)} %get-tuple-element.122), channel_id=1, replica_groups=mesh['ctx'=32,'head'=8] {'head'}, use_global_device_ids=true, to_apply=%region_1.0 | all-reduce | flops 512 | bytes 4096 | tf_op jit(solution)/shard_map/psum | solution.py:62
  40.0 312.7 %all-reduce.4.cloned.1.call-done = (bf16[1,2,1024,640]{2,3,1,0:T(8,128)(2,1)}, bf16[1,2,1024,640]{2,3,1,0:T(8,128)(2,1)}) async-done(((bf16[1,2,1024,640]{2,3,1,0:T(8,128)(2,1)}, bf16[1,2,1024,640]{2,3,1,0:T(8,128)(2,1)}), (bf16[1,2,1024,640]{2,3,1,0:T(8,128)(2,1)}, bf16[1,2,1024,640]{2,3,1,0:T(8,128)(2,1)})) %all-reduce.4.cloned.1.call-update) | async-done | bytes 5242896 | tf_op jit(solution)/shard_map/psum | solution.py:16
  352.6 5.3 pad_maximum_fusion
  358.0 168.4 %all-gather.5.cloned.1.call-done = bf16[8192,640]{1,0:T(8,128)(2,1)} async-done(((bf16[256,640]{1,0:T(8,128)(2,1)}), bf16[8192,640]{1,0:T(8,128)(2,1)}) %all-gather.5.cloned.1.call-update) | async-done | bytes 10485776 | tf_op jit(solution)/shard_map/all_gather | solution.py:72
  526.4 7.2 gather_fusion.1
  533.6 166.6 %all-gather.3.cloned.1.call-done = bf16[8192,640]{1,0:T(8,128)(2,1)} async-done(((bf16[256,640]{1,0:T(8,128)(2,1)}), bf16[8192,640]{1,0:T(8,128)(2,1)}) %all-gather.3.cloned.1.call-update) | async-done | bytes 10485776 | tf_op jit(solution)/shard_map/all_gather | solution.py:73
  700.3 7.2 gather_fusion
  707.5 75.3 %while.10 = (s32[]{:T(128)}, bf16[2,128,640]{2,1,0:T(8,128)(2,1)}, s32[2]{0:T(128)S(1)}, bf16[2,128,640]{2,1,0:T(8,128)(2,1)}, s32[2]{0:T(128)S(1)}, /*index=5*/...) while((s32[]{:T(128)}, bf16[2,128,640]{2,1,0:T(8,128)(2,1)}, ...), condition=%wide.region_9.10_spmd, body=%wide.region_6.9_spmd.sunk | while | flops 915372800 | bytes 109458328 | solution.py:97
  712.5 4.4 constant_dynamic-slice_fusion.14
  717.0 2.7 copy.74
  719.7 2.3 copy.75
  721.9 3.0 constant_dynamic-slice_fusion.13
  725.0 1.5 copy.73
  728.0 4.5 multiply_reduce_fusion.2
  733.8 1.7 copy-done.3
  735.5 2.4 copy.78
  739.1 5.1 fusion.55
  750.2 4.4 constant_dynamic-slice_fusion.14
  754.6 2.7 copy.74
  757.3 2.3 copy.75
  759.6 3.0 constant_dynamic-slice_fusion.13
  765.6 4.5 multiply_reduce_fusion.2
  771.4 1.7 copy-done.3
  773.2 2.4 copy.78
  776.7 5.1 fusion.55
  782.8 5.2 convolution_convert_fusion
  788.0 2.6 copy.54
  790.6 49.1 %reduce-scatter.4.cloned.1.call-done = bf16[640,256]{1,0:T(8,128)(2,1)} async-done(((bf16[5120,256]{1,0:T(8,128)(2,1)}), bf16[640,256]{1,0:T(8,128)(2,1)}) %reduce-scatter.4.cloned.1.call-update) | async-done | bytes 327696
  839.7 1.9 copy.55
  (80 shorter events, 19.0 us)
Async XLA Ops:
  7.2 31.6 %copy-start = (s32[32,2,12]{0,1,2:T(2,128)S(1)}, s32[32,2,12]{0,1,2:T(2,128)}, u32[]{:S(2)}) copy-start(s32[32,2,12]{0,1,2:T(2,128)} %param.21) | copy-start | bytes 9220
  7.2 345.5 %all-reduce.4.cloned.1.call-start = ((), (), s32[]{:S(2)}) async-start(), calls=%async_computation.4 | async-start | bytes 10485760 | tf_op jit(solution)/shard_map/psum | solution.py:16
  15.8 1.0 copy-start.6
  15.8 1.1 copy-start.7
  15.8 21.2 %copy-start.8 = (f32[640]{0:T(1024)S(1)}, f32[640]{0:T(1024)}, u32[]{:S(2)}) copy-start(f32[640]{0:T(1024)} %param.17) | copy-start | bytes 7684
  15.8 23.2 %copy-start.9 = (f32[640]{0:T(1024)S(1)}, f32[640]{0:T(1024)}, u32[]{:S(2)}) copy-start(f32[640]{0:T(1024)} %param.16) | copy-start | bytes 7684
  15.9 510.5 %all-gather.5.cloned.1.call-start = ((), (), s32[]{:S(2)}) async-start(), calls=%async_computation.2 | async-start | bytes 10813440 | tf_op jit(solution)/shard_map/all_gather | solution.py:72
  38.0 662.3 %all-gather.3.cloned.1.call-start = ((), (), s32[]{:S(2)}) async-start(), calls=%async_computation.1 | async-start | bytes 10813440 | tf_op jit(solution)/shard_map/all_gather | solution.py:73
  38.7 801.0 %reduce-scatter.4.cloned.1.call-start = ((), (), s32[]{:S(2)}) async-start(), calls=%async_computation.3 | async-start | bytes 2949120
  700.3 7.3 copy-start.12
  725.0 3.0 copy-start.4
  732.5 3.0 copy-start.3
  732.5 3.0 copy-start.2
  735.5 3.6 copy-start.5
  739.0 5.3 copy-start.10
  744.4 0.7 copy-start.11
  762.6 3.0 copy-start.4
  770.1 3.0 copy-start.3
  770.1 3.0 copy-start.2
  773.1 3.6 copy-start.5
  776.7 5.3 copy-start.10
  782.1 0.7 copy-start.11
  782.8 58.8 %copy-start.1 = (s32[32,2,12]{0,1,2:T(2,128)S(1)}, s32[32,2,12]{0,1,2:T(2,128)}, u32[]{:S(2)}) copy-start(s32[32,2,12]{0,1,2:T(2,128)} %param.21) | copy-start | bytes 9220
Sparse Core Ops, SparseCore 0:
  16.0 336.6 all-reduce.3
  354.4 171.9 all-gather.4
  528.2 172.0 all-gather.2
  790.7 48.9 reduce-scatter.3
where the time goes:
time: 849 us; the launch traced here: 848 us
  waiting for transfers between devices  698 us (82%)
  local copies, waits for them, and re-layouts  70.4 us (8%)
  matrix products  24.5 us (3%)
  blocking collectives  19.9 us (2%)
  between operations  15.2 us (2%)
  other arithmetic  12.6 us (1%)
    psum x1, waiting for transfers between devices, spread(): return lax.psum(kept, axis)  313 us
    all_gather x1, waiting for transfers between devices, shards(): lax.all_gather(k_norm, 'ctx', axis=0, tiled=True)  168 us
    all_gather x1, waiting for transfers between devices, shards(): lax.all_gather(values, 'ctx', axis=0, tiled=True)  167 us
    unnamed x5, waiting for transfers between devices  49.9 us
    psum x1, blocking collectives, shards(): lax.psum((jnp.sum(q_float * q_float, axis=1), jnp.sum(k_float * k_float,...  19.9 us
  transfers between devices with their start and end apart: 4, of which 4 were waited for; matrix products, arithmetic and copies ran while one was open for 2% of the time, Pallas kernels for 0%

commit v1 on v0

--- a/solution.py
+++ b/solution.py
@@ -9,11 +9,6 @@
 
 
 epsilon = 1e-06
-
-
-def spread(value, axis, source):
-    kept = jnp.where(lax.axis_index(axis) == source, value, 0).astype(value.dtype)
-    return lax.psum(kept, axis)
 
 
 def normalize(features, scale_gain, square_total):
@@ -55,8 +50,11 @@
 ):
     tokens, width = queries.shape
     blocks = tokens // BLK
+    n_ctx = partners.shape[0]
+    persons = partners.shape[1]
+    bank_rows = ref_keys.shape[0]
+    piece = bank_rows // n_ctx
     own_index = lax.axis_index("ctx")
-    persons = partners.shape[1]
     q_float = queries.astype(jnp.float32)
     k_float = keys.astype(jnp.float32)
     q_total, k_total = lax.psum(
@@ -67,20 +65,26 @@
     query_blocks = q_norm.reshape(blocks, BLK, width)
     key_blocks = k_norm.reshape(blocks, BLK, width)
     value_blocks = values.reshape(blocks, BLK, width)
-    wanted = partners[own_index].reshape(-1)
-    whole_keys, whole_values = (
-        lax.all_gather(k_norm, "ctx", axis=0, tiled=True),
-        lax.all_gather(values, "ctx", axis=0, tiled=True),
+
+    flat = partners.reshape(n_ctx, -1)
+    hit = (flat // blocks) == own_index
+    pick = jnp.sum(jnp.where(hit, flat % blocks, 0), axis=1)
+    kv_blocks = jnp.stack([key_blocks, value_blocks], axis=1)
+    send_blocks = kv_blocks[pick]
+    bank = jnp.stack([ref_keys, ref_values]).reshape(2, n_ctx, piece, width)
+    send_bank = jnp.transpose(bank, (1, 0, 2, 3))
+    send = jnp.concatenate([send_blocks, send_bank], axis=2)
+    got = lax.all_to_all(send, "ctx", 0, 0, tiled=True)
+    got_blocks = got[:, :, :BLK]
+    got_bank = got[:, :, BLK:]
+
+    wanted = partners[own_index]
+    far = got_blocks[wanted // blocks]
+    far = far.transpose(0, 2, 1, 3, 4).reshape(persons, 2, -1, width)
+    mine = got_bank[owners]
+    identity = jnp.transpose(lax.all_gather(mine, "ctx", axis=0, tiled=False), (1, 2, 0, 3, 4)).reshape(
+        persons, 2, bank_rows, width
     )
-    far_keys = whole_keys.reshape(-1, BLK, width)[wanted]
-    far_values = whole_values.reshape(-1, BLK, width)[wanted]
-    far_keys = far_keys.reshape(persons, -1, width)
-    far_values = far_values.reshape(persons, -1, width)
-    local_bank = jnp.stack([ref_keys, ref_values])
-    identities = []
-    for person in range(persons):
-        identities.append(spread(local_bank, "ctx", owners[person]))
-    identity_stack = jnp.stack(identities)
 
     def one_block(position):
         person_label = labels[position]
@@ -88,10 +92,10 @@
             query_blocks[position],
             key_blocks[position],
             value_blocks[position],
-            far_keys[person_label],
-            far_values[person_label],
-            identity_stack[person_label, 0],
-            identity_stack[person_label, 1],
+            far[person_label, 0],
+            far[person_label, 1],
+            identity[person_label, 0],
+            identity[person_label, 1],
         )
 
     attended = lax.map(one_block, jnp.arange(blocks)).reshape(tokens, width)

time: 849 us -> 572 us (0.67)
  waiting for transfers between devices: 698 us -> 388 us
  local copies, waits for them, and re-layouts: 70.4 us -> 97.3 us
  matrix products: 24.5 us -> 14 us
    psum x1 -> x0, waiting for transfers between devices: 313 us -> none  [spread(): return lax.psum(kept, axis)]
    all_to_all x0 -> x1, waiting for transfers between devices: none -> 184 us  [shards(): got = lax.all_to_all(send, 'ctx', 0, 0, tiled=True)]
    all_gather x2 -> x1, waiting for transfers between devices: 335 us -> 155 us  [shards(): lax.all_gather(mine, 'ctx', axis=0, tiled=False)]
    while x24 -> x26, local copies, waits for them, and re-layouts: 4.97 us -> 21.4 us  [the longest x2 18.6 us: shards(): attended = lax.map(one_block, jnp.arange(blocks)).reshape(tokens, width)]
    transpose x0 -> x2, local copies, waits for them, and re-layouts: none -> 13 us  [the longest x1 7.61 us: shards(): far = far.transpose(0, 2, 1, 3, 4).reshape(persons, 2, -1, width)]
    dynamic_slice x10 -> x6, local copies, waits for them, and re-layouts: 25.3 us -> 13.6 us  [the longest x2 7.33 us: one_block(): far[person_label, 1]]
    slice x1 -> x2, local copies, waits for them, and re-layouts: 1.31 us -> 11.5 us  [the longest x1 9.57 us: shards(): got_blocks = got[:, :, :BLK]]
    concatenate x0 -> x1, other arithmetic: none -> 10 us  [shards(): send = jnp.concatenate([send_blocks, send_bank], axis=2)]
  transfers between devices with their start and end apart: 4 -> 3, of which waited for: 4 -> 3; matrix products, arithmetic and copies ran while one was open for 2% -> 7% of each run, Pallas kernels for 0% -> 0%
where the time goes in v1:
time: 572 us; the launch traced here: 570 us
  waiting for transfers between devices  388 us (68%)
  local copies, waits for them, and re-layouts  97.3 us (17%)
  other arithmetic  20 us (3%)
  blocking collectives  19.9 us (3%)
  between operations  14.2 us (2%)
  matrix products  14 us (2%)
  starting transfers between devices  8.59 us (2%)
  loops' own time  8.29 us (1%)
    all_to_all x1, waiting for transfers between devices, shards(): got = lax.all_to_all(send, 'ctx', 0, 0, tiled=True)  184 us
    all_gather x1, waiting for transfers between devices, shards(): lax.all_gather(mine, 'ctx', axis=0, tiled=False)  155 us
    unnamed x3, waiting for transfers between devices  48.7 us
    psum x1, blocking collectives, shards(): lax.psum((jnp.sum(q_float * q_float, axis=1), jnp.sum(k_float * k_float,...  19.9 us
    while x2, local copies, waits for them, and re-layouts, shards(): attended = lax.map(one_block, jnp.arange(blocks)).reshape(tokens, width)  18.6 us
  transfers between devices with their start and end apart: 3, of which 3 were waited for; matrix products, arithmetic and copies ran while one was open for 7% of the time, Pallas kernels for 0%

profile of v1, /device:TPU:2, one launch (start us, length us, event | category | flops | bytes accessed | tf_op | source)
XLA Modules:
  0.0 570.1 jit_solution(15789934079374993929)
XLA Ops:
  10.2 19.9 %all-reduce = (f32[256]{0:T(256)S(1)}, f32[256]{0:T(256)S(1)}) all-reduce(f32[256]{0:T(256)S(1)} %fusion.35, f32[256]{0:T(256)S(1)} %fusion.38), channel_id=1, replica_groups=mesh['ctx'=32,'head'=8] {'head'}, use_global_device_ids=true, to_apply=%region_3.0 | all-reduce | flops 512 | bytes 4096 | tf_op jit(solution)/shard_map/psum | solution.py:60
  32.5 2.0 maximum_bitcast_fusion
  34.5 5.9 %gather_fusion = bf16[32,2,128,640]{3,2,1,0:T(8,128)(2,1)} fusion(bf16[2,2,128,640]{3,2,0,1:T(8,128)(2,1)S(1)} %pad_maximum_fusion.1, s32[1024]{0:T(1024)S(1)} %pad_clamp_fusion.2), kind=kCustom, calls=%fused_computation | custom fusion | bytes 20971648 | tf_op jit(solution)/shard_map/gather | solution.py:73
  40.4 10.0 %pad_maximum_fusion = bf16[32,2,160,640]{3,2,1,0:T(8,128)(2,1)} fusion(bf16[32,2,32,640]{3,2,1,0:T(8,128)(2,1)S(1)} %maximum_bitcast_fusion, bf16[32,2,128,640]{3,2,1,0:T(8,128)(2,1)} %gather_fusion), kind=kLoop, calls=%fused_computation.35 | loop fusion | flops 26214400 | bytes 26214400 | tf_op jit(solution)/shard_map/concatenate | solution.py:76
  50.4 8.3 %all-to-all-start = ((bf16[32,2,160,640]{3,2,1,0:T(8,128)(2,1)}), bf16[32,2,160,640]{3,2,1,0:T(8,128)(2,1)}, u32[]{:S(2)}, u32[]{:S(2)}) async-start(bf16[32,2,160,640]{3,2,1,0:T(8,128)(2,1)} %pad_maximum_fusion), calls=%async_computation | async-start | bytes 26214400 | tf_op jit(solution)/shard_map/all_to_all | solution.py:77
  58.9 184.5 %all-to-all-done = bf16[32,2,160,640]{3,2,1,0:T(8,128)(2,1)} async-done(((bf16[32,2,160,640]{3,2,1,0:T(8,128)(2,1)}), bf16[32,2,160,640]{3,2,1,0:T(8,128)(2,1)}, u32[]{:S(2)}, u32[]{:S(2)}) %all-to-all-start) | async-done | bytes 13107232 | tf_op jit(solution)/shard_map/all_to_all | solution.py:77
  243.3 2.0 slice.15
  245.3 1.2 gather_fusion.2
  247.3 9.6 %slice.14 = bf16[32,2,128,640]{3,2,1,0:T(8,128)(2,1)} slice(bf16[32,2,160,640]{3,2,1,0:T(8,128)(2,1)} %all-to-all-done), slice={[0:32], [0:2], [0:128], [0:640]} | slice | bytes 20971520 | tf_op jit(solution)/shard_map/slice | solution.py:78
  256.8 9.2 %gather_fusion.1 = bf16[24,2,128,640]{3,2,1,0:T(8,128)(2,1)} fusion(bf16[32,2,128,640]{3,2,1,0:T(8,128)(2,1)} %slice.14, s32[1024]{0:T(1024)S(1)} %pad_clamp_fusion.1), kind=kCustom, calls=%fused_computation.1 | custom fusion | bytes 15728736 | tf_op jit(solution)/shard_map/gather | solution.py:82
  266.1 7.6 %copy.50 = bf16[2,2,12,128,640]{4,3,2,1,0:T(8,128)(2,1)} copy(bf16[2,2,12,128,640]{4,3,1,2,0:T(8,128)(2,1)} %bitcast.90) | data formatting | bytes 15728640 | tf_op jit(solution)/shard_map/transpose | solution.py:83
  273.7 10.7 %copy.53 = bf16[2,2,1536,640]{2,3,1,0:T(8,128)(2,1)} copy(bf16[2,2,1536,640]{3,2,1,0:T(8,128)(2,1)} %bitcast.91) | data formatting | bytes 15728640 | tf_op jit(solution)/shard_map/while | solution.py:101
  284.4 154.5 %all-gather.3.cloned.1.call-done = bf16[64,2,32,640]{3,2,1,0:T(8,128)(2,1)} async-done(((bf16[2,2,32,640]{3,2,1,0:T(8,128)(2,1)}), bf16[64,2,32,640]{3,2,1,0:T(8,128)(2,1)}) %all-gather.3.cloned.1.call-update) | async-done | bytes 5242896 | tf_op jit(solution)/shard_map/all_gather | solution.py:85
  438.9 5.4 copy.51
  444.2 7.9 %copy.54 = bf16[2,2,1024,640]{2,3,1,0:T(8,128)(2,1)} copy(bf16[2,2,1024,640]{3,2,1,0:T(8,128)(2,1)} %bitcast.92) | data formatting | bytes 10485760 | tf_op jit(solution)/shard_map/while | solution.py:101
  452.2 52.7 %while.10 = (s32[]{:T(128)}, bf16[2,128,640]{2,1,0:T(8,128)(2,1)}, s32[2]{0:T(128)S(1)}, bf16[2,128,640]{2,1,0:T(8,128)(2,1)}, s32[2]{0:T(128)S(1)}, /*index=5*/...) while((s32[]{:T(128)}, bf16[2,128,640]{2,1,0:T(8,128)(2,1)}, ...), condition=%wide.region_8.9_spmd, body=%wide.region_5.8_spmd.sunk | while | flops 915372800 | bytes 68826000 | solution.py:101
  461.5 3.0 constant_dynamic-slice_fusion.13
  465.3 3.7 constant_dynamic-slice_fusion.14
  468.9 2.3 copy.75
  471.2 2.9 multiply_reduce_fusion.2
  474.1 1.2 fusion.54
  476.0 1.5 fusion.55
  487.8 3.0 constant_dynamic-slice_fusion.13
  491.6 3.7 constant_dynamic-slice_fusion.14
  495.3 2.3 copy.75
  497.6 2.9 multiply_reduce_fusion.2
  500.5 1.2 fusion.54
  502.4 1.5 fusion.55
  504.9 5.2 convolution_convert_fusion
  510.1 2.6 copy.59
  512.6 48.7 %reduce-scatter.4.cloned.1.call-done = bf16[640,256]{1,0:T(8,128)(2,1)} async-done(((bf16[5120,256]{1,0:T(8,128)(2,1)}), bf16[640,256]{1,0:T(8,128)(2,1)}) %reduce-scatter.4.cloned.1.call-update) | async-done | bytes 327696
  561.3 1.9 copy.60
  (80 shorter events, 21.2 us)
Async XLA Ops:
  31.3 1.2 copy-start.2
  50.4 8.4 %copy-start.10 = (s32[2]{0:T(128)S(1)}, s32[2]{0:T(128)}, u32[]{:S(2)}) copy-start(s32[2]{0:T(128)} %param.22) | copy-start | bytes 28
  50.4 196.4 %copy-start.6 = (s32[32,2,12]{0,1,2:T(2,128)S(1)}, s32[32,2,12]{0,1,2:T(2,128)}, u32[]{:S(2)}) copy-start(s32[32,2,12]{0,1,2:T(2,128)} %param.21) | copy-start | bytes 9220
  50.4 196.7 %copy-start.5 = (bf16[256,640]{1,0:T(8,128)(2,1)S(1)}, bf16[256,640]{1,0:T(8,128)(2,1)}, u32[]{:S(2)}) copy-start(bf16[256,640]{1,0:T(8,128)(2,1)} %param.13) | copy-start | bytes 983044
  50.4 196.7 %copy-start.7 = (f32[640]{0:T(1024)S(1)}, f32[640]{0:T(1024)}, u32[]{:S(2)}) copy-start(f32[640]{0:T(1024)} %param.16) | copy-start | bytes 7684
  50.4 192.9 %all-to-all-start = ((bf16[32,2,160,640]{3,2,1,0:T(8,128)(2,1)}), bf16[32,2,160,640]{3,2,1,0:T(8,128)(2,1)}, u32[]{:S(2)}, u32[]{:S(2)}) async-start(bf16[32,2,160,640]{3,2,1,0:T(8,128)(2,1)} %pad_maximum_fusion), calls=%async_computation | async-start | bytes 26214400 | tf_op jit(solution)/shard_map/all_to_all | solution.py:77
  58.8 380.1 %all-gather.3.cloned.1.call-start = ((), (), s32[]{:S(2)}) async-start(), calls=%async_computation.2 | async-start | bytes 5406720 | tf_op jit(solution)/shard_map/all_gather | solution.py:85
  246.6 314.8 %reduce-scatter.4.cloned.1.call-start = ((), (), s32[]{:S(2)}) async-start(), calls=%async_computation.3 | async-start | bytes 2949120
  444.2 7.9 %copy-start.11 = (s32[2]{0:T(128)S(1)}, s32[2]{0:T(128)}, u32[]{:S(2)}) copy-start(s32[2]{0:T(128)} %param.23) | copy-start | bytes 28
  452.2 8.5 %copy-start.3 = (bf16[2,128,640]{2,1,0:T(8,128)(2,1)}, bf16[2,128,640]{2,1,0:T(8,128)(2,1)S(1)}, u32[]{:S(2)}) copy-start(bf16[2,128,640]{2,1,0:T(8,128)(2,1)S(1)} %get-tuple-element.209) | copy-start | bytes 983044 | tf_op jit(solution)/shard_map/while
  474.1 1.6 copy-start
  474.1 1.9 copy-start.1
  476.0 1.7 copy-start.8
  476.0 2.5 copy-start.4
  477.8 0.7 copy-start.9
  478.5 8.5 %copy-start.3 = (bf16[2,128,640]{2,1,0:T(8,128)(2,1)}, bf16[2,128,640]{2,1,0:T(8,128)(2,1)S(1)}, u32[]{:S(2)}) copy-start(bf16[2,128,640]{2,1,0:T(8,128)(2,1)S(1)} %get-tuple-element.209) | copy-start | bytes 983044 | tf_op jit(solution)/shard_map/while
  500.5 1.6 copy-start
  500.5 1.9 copy-start.1
  502.4 1.7 copy-start.8
  502.4 2.5 copy-start.4
  504.1 0.7 copy-start.9
Sparse Core Ops, SparseCore 0:
  246.7 192.1 all-gather.2
  512.8 48.5 reduce-scatter.3

commit v2 on v1

--- a/solution.py
+++ b/solution.py
@@ -1,7 +1,13 @@
+import functools
+
 import jax
 import jax.numpy as jnp
 from jax import lax
+from jax.experimental import pallas as pl
+from jax.experimental.pallas import tpu as pltpu
 from jax.sharding import PartitionSpec as P
+
+MESH = pl.DeviceIdType.MESH
 
 D = 5120
 HD = 128
@@ -9,6 +15,61 @@
 
 
 epsilon = 1e-06
+
+
+def gather_kernel(axis, other_axis, n, piece_ref, out_ref, send_sem, recv_sem, local_sem):
+    me = lax.axis_index(axis)
+    other = lax.axis_index(other_axis)
+
+    def device(j):
+        return (j, other) if axis == "ctx" else (other, j)
+
+    barrier = pltpu.get_barrier_semaphore()
+    for k in range(1, n):
+        pl.semaphore_signal(barrier, inc=1, device_id=device(lax.rem(me + k, n)), device_id_type=MESH)
+    pl.semaphore_wait(barrier, n - 1)
+    local = pltpu.make_async_copy(piece_ref, out_ref.at[me], local_sem)
+    local.start()
+    sends = []
+    for k in range(1, n):
+        copy = pltpu.make_async_remote_copy(
+            src_ref=piece_ref,
+            dst_ref=out_ref.at[me],
+            send_sem=send_sem.at[k],
+            recv_sem=recv_sem.at[k],
+            device_id=device(lax.rem(me + k, n)),
+            device_id_type=MESH,
+        )
+        copy.start()
+        sends.append(copy)
+    local.wait()
+    for copy in sends:
+        copy.wait_send()
+    for k in range(1, n):
+        source = lax.rem(me + n - k, n)
+        pltpu.make_async_remote_copy(
+            src_ref=piece_ref,
+            dst_ref=out_ref.at[source],
+            send_sem=send_sem.at[k],
+            recv_sem=recv_sem.at[k],
+            device_id=device(source),
+            device_id_type=MESH,
+        ).wait_recv()
+
+
+def gather_all(piece, axis, other_axis, n, collective_id):
+    return pl.pallas_call(
+        functools.partial(gather_kernel, axis, other_axis, n),
+        out_shape=jax.ShapeDtypeStruct((n,) + piece.shape, piece.dtype),
+        in_specs=[pl.BlockSpec(memory_space=pl.ANY)],
+        out_specs=pl.BlockSpec(memory_space=pl.ANY),
+        scratch_shapes=[
+            pltpu.SemaphoreType.DMA((n,)),
+            pltpu.SemaphoreType.DMA((n,)),
+            pltpu.SemaphoreType.DMA(()),
+        ],
+        compiler_params=pltpu.CompilerParams(collective_id=collective_id, has_side_effects=True),
+    )(piece)
 
 
 def normalize(features, scale_gain, square_total):
@@ -57,9 +118,9 @@
     own_index = lax.axis_index("ctx")
     q_float = queries.astype(jnp.float32)
     k_float = keys.astype(jnp.float32)
-    q_total, k_total = lax.psum(
-        (jnp.sum(q_float * q_float, axis=1), jnp.sum(k_float * k_float, axis=1)), "head"
-    )
+    n_head = lax.axis_size("head")
+    squares = jnp.stack([jnp.sum(q_float * q_float, axis=1), jnp.sum(k_float * k_float, axis=1)])
+    q_total, k_total = jnp.sum(gather_all(squares, "head", "ctx", n_head, 1), axis=0)
     q_norm = normalize(q_float, q_gain, q_total)
     k_norm = normalize(k_float, k_gain, k_total)
     query_blocks = q_norm.reshape(blocks, BLK, width)
@@ -82,7 +143,8 @@
     far = got_blocks[wanted // blocks]
     far = far.transpose(0, 2, 1, 3, 4).reshape(persons, 2, -1, width)
     mine = got_bank[owners]
-    identity = jnp.transpose(lax.all_gather(mine, "ctx", axis=0, tiled=False), (1, 2, 0, 3, 4)).reshape(
+    whole = gather_all(mine.reshape(-1, width), "ctx", "head", n_ctx, 2)
+    identity = jnp.transpose(whole.reshape((n_ctx,) + mine.shape), (1, 2, 0, 3, 4)).reshape(
         persons, 2, bank_rows, width
     )
 

time: 572 us -> 549 us (0.960)
  waiting for transfers between devices: 388 us -> 262 us
  Pallas kernels: 0 us -> 121 us
  blocking collectives: 19.9 us -> 0 us
    all_gather x1 -> x0, waiting for transfers between devices: 155 us -> none  [shards(): lax.all_gather(mine, 'ctx', axis=0, tiled=False)]
    pallas_call x0 -> x2, Pallas kernels: none -> 121 us  [gather_all(): pl.pallas_call(functools.partial(gather_kernel, axis, other_axis, n), out...]
    psum x1 -> x0, blocking collectives: 19.9 us -> none  [shards(): lax.psum((jnp.sum(q_float * q_float, axis=1), jnp.sum(k_float * k_float,...]
    unnamed x3 -> x2, waiting for transfers between devices: 48.7 us -> 64.9 us
    all_to_all x1, waiting for transfers between devices: 184 us -> 197 us  [shards(): got = lax.all_to_all(send, 'ctx', 0, 0, tiled=True)]
  transfers between devices with their start and end apart: 3 -> 2, of which waited for: 3 -> 2; matrix products, arithmetic and copies ran while one was open for 7% -> 0% of each run, Pallas kernels for 0% -> 0%
where the time goes in v2:
time: 549 us; the launch traced here: 547 us
  waiting for transfers between devices  262 us (48%)
  Pallas kernels  121 us (22%)
  local copies, waits for them, and re-layouts  97.7 us (18%)
  other arithmetic  21.3 us (4%)
  between operations  14.2 us (3%)
  matrix products  14 us (3%)
  loops' own time  8.29 us (2%)
  starting transfers between devices  8.2 us (1%)
    all_to_all x1, waiting for transfers between devices, shards(): got = lax.all_to_all(send, 'ctx', 0, 0, tiled=True)  197 us
    pallas_call x2, Pallas kernels, gather_all(): pl.pallas_call(functools.partial(gather_kernel, axis, other_axis, n), out...  121 us
    unnamed x2, waiting for transfers between devices  64.9 us
    while x2, local copies, waits for them, and re-layouts, shards(): attended = lax.map(one_block, jnp.arange(blocks)).reshape(tokens, width)  18.6 us
  transfers between devices with their start and end apart: 2, of which 2 were waited for; matrix products, arithmetic and copies ran while one was open for 0% of the time, Pallas kernels for 0%

profile of v2, /device:TPU:2, one launch (start us, length us, event | category | flops | bytes accessed | tf_op | source)
XLA Modules:
  0.0 546.6 jit_solution(5296171087922798334)
XLA Ops:
  10.8 10.9 %shard_map.122 = f32[8,2,256]{2,1,0:T(2,128)} custom-call(f32[2,256]{1,0:T(2,128)} %pad_maximum_fusion.2.piece_ref), custom_call_target="tpu_custom_call" | custom-call | tf_op jit(solution)/shard_map/pallas_call | solution.py:61
  24.7 2.0 maximum_bitcast_fusion
  26.7 6.0 %gather_fusion = bf16[32,2,128,640]{3,2,1,0:T(8,128)(2,1)} fusion(bf16[2,2,128,640]{3,2,0,1:T(8,128)(2,1)S(1)} %pad_maximum_fusion.1, s32[1024]{0:T(1024)S(1)} %pad_clamp_fusion.2), kind=kCustom, calls=%fused_computation | custom fusion | bytes 20971648 | tf_op jit(solution)/shard_map/gather | solution.py:134
  32.8 10.0 %pad_maximum_fusion = bf16[32,2,160,640]{3,2,1,0:T(8,128)(2,1)} fusion(bf16[32,2,32,640]{3,2,1,0:T(8,128)(2,1)S(1)} %maximum_bitcast_fusion, bf16[32,2,128,640]{3,2,1,0:T(8,128)(2,1)} %gather_fusion), kind=kLoop, calls=%fused_computation.35 | loop fusion | flops 26214400 | bytes 26214400 | tf_op jit(solution)/shard_map/concatenate | solution.py:137
  42.8 8.2 %all-to-all-start = ((bf16[32,2,160,640]{3,2,1,0:T(8,128)(2,1)}), bf16[32,2,160,640]{3,2,1,0:T(8,128)(2,1)}, u32[]{:S(2)}, u32[]{:S(2)}) async-start(bf16[32,2,160,640]{3,2,1,0:T(8,128)(2,1)} %pad_maximum_fusion), calls=%async_computation | async-start | bytes 26214400 | tf_op jit(solution)/shard_map/all_to_all | solution.py:138
  51.5 197.1 %all-to-all-done = bf16[32,2,160,640]{3,2,1,0:T(8,128)(2,1)} async-done(((bf16[32,2,160,640]{3,2,1,0:T(8,128)(2,1)}), bf16[32,2,160,640]{3,2,1,0:T(8,128)(2,1)}, u32[]{:S(2)}, u32[]{:S(2)}) %all-to-all-start) | async-done | bytes 13107232 | tf_op jit(solution)/shard_map/all_to_all | solution.py:138
  248.6 9.6 %slice.14 = bf16[32,2,128,640]{3,2,1,0:T(8,128)(2,1)} slice(bf16[32,2,160,640]{3,2,1,0:T(8,128)(2,1)} %all-to-all-done), slice={[0:32], [0:2], [0:128], [0:640]} | slice | bytes 20971520 | tf_op jit(solution)/shard_map/slice | solution.py:139
  258.3 9.5 %gather_fusion.1 = bf16[24,2,128,640]{3,2,1,0:T(8,128)(2,1)} fusion(bf16[32,2,128,640]{3,2,1,0:T(8,128)(2,1)} %slice.14, s32[1024]{0:T(1024)S(1)} %pad_clamp_fusion.1), kind=kCustom, calls=%fused_computation.1 | custom fusion | bytes 15728736 | tf_op jit(solution)/shard_map/gather | solution.py:143
  267.7 7.6 %copy.51 = bf16[2,2,12,128,640]{4,3,2,1,0:T(8,128)(2,1)} copy(bf16[2,2,12,128,640]{4,3,1,2,0:T(8,128)(2,1)} %bitcast.95) | data formatting | bytes 15728640 | tf_op jit(solution)/shard_map/transpose | solution.py:144
  275.3 10.7 %copy.54 = bf16[2,2,1536,640]{2,3,1,0:T(8,128)(2,1)} copy(bf16[2,2,1536,640]{3,2,1,0:T(8,128)(2,1)} %bitcast.96) | data formatting | bytes 15728640 | tf_op jit(solution)/shard_map/while | solution.py:163
  286.0 2.0 slice.15
  288.0 1.2 gather_fusion.2
  289.2 110.0 %shard_map.123 = bf16[32,128,640]{2,1,0:T(8,128)(2,1)} custom-call(bf16[128,640]{1,0:T(8,128)(2,1)} %bitcast.109), custom_call_target="tpu_custom_call" | custom-call | tf_op jit(solution)/shard_map/pallas_call | solution.py:61
  399.3 5.4 copy.52
  404.6 7.9 %copy.55 = bf16[2,2,1024,640]{2,3,1,0:T(8,128)(2,1)} copy(bf16[2,2,1024,640]{3,2,1,0:T(8,128)(2,1)} %bitcast.98) | data formatting | bytes 10485760 | tf_op jit(solution)/shard_map/while | solution.py:163
  412.6 52.7 %while.10 = (s32[]{:T(128)}, bf16[2,128,640]{2,1,0:T(8,128)(2,1)}, s32[2]{0:T(128)S(1)}, bf16[2,128,640]{2,1,0:T(8,128)(2,1)}, s32[2]{0:T(128)S(1)}, /*index=5*/...) while((s32[]{:T(128)}, bf16[2,128,640]{2,1,0:T(8,128)(2,1)}, ...), condition=%wide.region_7.8_spmd, body=%wide.region_4.7_spmd.sunk | while | flops 915372800 | bytes 68826000 | solution.py:163
  421.8 3.0 constant_dynamic-slice_fusion.13
  425.6 3.7 constant_dynamic-slice_fusion.14
  429.3 2.3 copy.76
  431.6 2.9 multiply_reduce_fusion.2
  434.5 1.2 fusion.58
  436.4 1.5 fusion.59
  448.2 3.0 constant_dynamic-slice_fusion.13
  452.0 3.7 constant_dynamic-slice_fusion.14
  455.7 2.3 copy.76
  458.0 2.9 multiply_reduce_fusion.2
  460.9 1.2 fusion.58
  462.8 1.5 fusion.59
  465.3 5.2 convolution_convert_fusion
  470.5 2.6 copy.60
  473.0 64.9 %reduce-scatter.4.cloned.1.call-done = bf16[640,256]{1,0:T(8,128)(2,1)} async-done(((bf16[5120,256]{1,0:T(8,128)(2,1)}), bf16[640,256]{1,0:T(8,128)(2,1)}) %reduce-scatter.4.cloned.1.call-update) | async-done | bytes 327696
  537.9 1.9 copy.61
  (80 shorter events, 22.2 us)
Async XLA Ops:
  23.5 1.2 copy-start.2
  42.8 8.2 %copy-start.6 = (s32[32,2,12]{0,1,2:T(2,128)S(1)}, s32[32,2,12]{0,1,2:T(2,128)}, u32[]{:S(2)}) copy-start(s32[32,2,12]{0,1,2:T(2,128)} %param.21) | copy-start | bytes 9220
  42.8 8.5 %copy-start.10 = (s32[2]{0:T(128)S(1)}, s32[2]{0:T(128)}, u32[]{:S(2)}) copy-start(s32[2]{0:T(128)} %param.22) | copy-start | bytes 28
  42.8 8.6 %copy-start.5 = (bf16[256,640]{1,0:T(8,128)(2,1)S(1)}, bf16[256,640]{1,0:T(8,128)(2,1)}, u32[]{:S(2)}) copy-start(bf16[256,640]{1,0:T(8,128)(2,1)} %param.13) | copy-start | bytes 983044
  42.8 8.6 %copy-start.7 = (f32[640]{0:T(1024)S(1)}, f32[640]{0:T(1024)}, u32[]{:S(2)}) copy-start(f32[640]{0:T(1024)} %param.16) | copy-start | bytes 7684
  42.8 205.8 %all-to-all-start = ((bf16[32,2,160,640]{3,2,1,0:T(8,128)(2,1)}), bf16[32,2,160,640]{3,2,1,0:T(8,128)(2,1)}, u32[]{:S(2)}, u32[]{:S(2)}) async-start(bf16[32,2,160,640]{3,2,1,0:T(8,128)(2,1)} %pad_maximum_fusion), calls=%async_computation | async-start | bytes 26214400 | tf_op jit(solution)/shard_map/all_to_all | solution.py:138
  51.0 486.9 %reduce-scatter.4.cloned.1.call-start = ((), (), s32[]{:S(2)}) async-start(), calls=%async_computation.2 | async-start | bytes 2949120
  404.6 7.9 %copy-start.11 = (s32[2]{0:T(128)S(1)}, s32[2]{0:T(128)}, u32[]{:S(2)}) copy-start(s32[2]{0:T(128)} %param.23) | copy-start | bytes 28
  412.6 8.4 %copy-start.3 = (bf16[2,128,640]{2,1,0:T(8,128)(2,1)}, bf16[2,128,640]{2,1,0:T(8,128)(2,1)S(1)}, u32[]{:S(2)}) copy-start(bf16[2,128,640]{2,1,0:T(8,128)(2,1)S(1)} %get-tuple-element.207) | copy-start | bytes 983044 | tf_op jit(solution)/shard_map/while
  434.5 1.6 copy-start
  434.5 1.9 copy-start.1
  436.4 1.7 copy-start.8
  436.4 2.5 copy-start.4
  438.2 0.7 copy-start.9
  438.9 8.4 %copy-start.3 = (bf16[2,128,640]{2,1,0:T(8,128)(2,1)}, bf16[2,128,640]{2,1,0:T(8,128)(2,1)S(1)}, u32[]{:S(2)}) copy-start(bf16[2,128,640]{2,1,0:T(8,128)(2,1)S(1)} %get-tuple-element.207) | copy-start | bytes 983044 | tf_op jit(solution)/shard_map/while
  460.9 1.6 copy-start
  460.9 1.9 copy-start.1
  462.8 1.7 copy-start.8
  462.8 2.5 copy-start.4
  464.5 0.7 copy-start.9
Sparse Core Ops, SparseCore 0:
  473.2 64.7 reduce-scatter.3

commit v3 on v2

--- a/solution.py
+++ b/solution.py
@@ -72,6 +72,84 @@
     )(piece)
 
 
+def attend_kernel(
+    label_ref, source_ref, q_ref, k_ref, v_ref, got_ref, whole_ref, o_ref,
+    far_k, far_v, bank_k, bank_v, sem_k, sem_v, sem_bank,
+):
+    position = pl.program_id(0)
+    person = label_ref[position]
+    far_count = far_k.shape[0] // BLK
+    piece = bank_k.shape[1]
+    copies = []
+    for j in range(far_count):
+        source = source_ref[person * far_count + j]
+        copies.append(pltpu.make_async_copy(
+            got_ref.at[source, 0, pl.ds(0, BLK)], far_k.at[pl.ds(j * BLK, BLK)], sem_k.at[j]))
+        copies.append(pltpu.make_async_copy(
+            got_ref.at[source, 1, pl.ds(0, BLK)], far_v.at[pl.ds(j * BLK, BLK)], sem_v.at[j]))
+    copies.append(pltpu.make_async_copy(
+        whole_ref.at[:, pl.ds(person * 2 * piece, piece)], bank_k, sem_bank.at[0]))
+    copies.append(pltpu.make_async_copy(
+        whole_ref.at[:, pl.ds(person * 2 * piece + piece, piece)], bank_v, sem_bank.at[1]))
+    for copy in copies:
+        copy.start()
+    for copy in copies:
+        copy.wait()
+    rows, width = q_ref.shape
+    bank_rows = bank_k.shape[0] * piece
+    dims = (((1,), (1,)), ((), ()))
+    for h in range(width // HD):
+        cols = pl.ds(h * HD, HD)
+        query = q_ref[:, cols]
+        parts = [
+            (k_ref[:, cols], v_ref[:, cols]),
+            (far_k[:, cols], far_v[:, cols]),
+            (bank_k[:, :, cols].reshape(bank_rows, HD), bank_v[:, :, cols].reshape(bank_rows, HD)),
+        ]
+        scores = [
+            lax.dot_general(query, key, dims, preferred_element_type=jnp.float32) * HD ** (-0.5)
+            for key, _ in parts
+        ]
+        peak = jnp.max(scores[0], axis=1, keepdims=True)
+        for score in scores[1:]:
+            peak = jnp.maximum(peak, jnp.max(score, axis=1, keepdims=True))
+        total = None
+        summed = None
+        for score, (_, value) in zip(scores, parts):
+            exponent = jnp.exp(score - peak)
+            part_sum = jnp.sum(exponent, axis=1, keepdims=True)
+            product = jnp.dot(exponent.astype(jnp.bfloat16), value, preferred_element_type=jnp.float32)
+            total = part_sum if total is None else total + part_sum
+            summed = product if summed is None else summed + product
+        o_ref[:, cols] = (summed / total).astype(o_ref.dtype)
+
+
+def attend(labels, sources, q_norm, k_norm, values, got, whole, n_ctx, far_count):
+    rows, width = q_norm.shape
+    piece = whole.shape[1] // 4
+    block = pl.BlockSpec((BLK, width), lambda b, lab, src: (b, 0))
+    return pl.pallas_call(
+        attend_kernel,
+        out_shape=jax.ShapeDtypeStruct((rows, width), jnp.bfloat16),
+        grid_spec=pltpu.PrefetchScalarGridSpec(
+            num_scalar_prefetch=2,
+            grid=(rows // BLK,),
+            in_specs=[block, block, block, pl.BlockSpec(memory_space=pl.ANY), pl.BlockSpec(memory_space=pl.ANY)],
+            out_specs=block,
+            scratch_shapes=[
+                pltpu.VMEM((far_count * BLK, width), jnp.bfloat16),
+                pltpu.VMEM((far_count * BLK, width), jnp.bfloat16),
+                pltpu.VMEM((n_ctx, piece, width), jnp.bfloat16),
+                pltpu.VMEM((n_ctx, piece, width), jnp.bfloat16),
+                pltpu.SemaphoreType.DMA((far_count,)),
+                pltpu.SemaphoreType.DMA((far_count,)),
+                pltpu.SemaphoreType.DMA((2,)),
+            ],
+        ),
+        compiler_params=pltpu.CompilerParams(dimension_semantics=("arbitrary",)),
+    )(labels, sources, q_norm, k_norm, values, got, whole)
+
+
 def normalize(features, scale_gain, square_total):
     factor = lax.rsqrt(square_total / D + epsilon)
     return (features * factor[:, None] * scale_gain[None, :]).astype(jnp.bfloat16)
@@ -136,31 +214,12 @@
     send_bank = jnp.transpose(bank, (1, 0, 2, 3))
     send = jnp.concatenate([send_blocks, send_bank], axis=2)
     got = lax.all_to_all(send, "ctx", 0, 0, tiled=True)
-    got_blocks = got[:, :, :BLK]
     got_bank = got[:, :, BLK:]
 
-    wanted = partners[own_index]
-    far = got_blocks[wanted // blocks]
-    far = far.transpose(0, 2, 1, 3, 4).reshape(persons, 2, -1, width)
+    sources = (partners[own_index] // blocks).reshape(-1)
     mine = got_bank[owners]
     whole = gather_all(mine.reshape(-1, width), "ctx", "head", n_ctx, 2)
-    identity = jnp.transpose(whole.reshape((n_ctx,) + mine.shape), (1, 2, 0, 3, 4)).reshape(
-        persons, 2, bank_rows, width
-    )
-
-    def one_block(position):
-        person_label = labels[position]
-        return attend_block(
-            query_blocks[position],
-            key_blocks[position],
-            value_blocks[position],
-            far[person_label, 0],
-            far[person_label, 1],
-            identity[person_label, 0],
-            identity[person_label, 1],
-        )
-
-    attended = lax.map(one_block, jnp.arange(blocks)).reshape(tokens, width)
+    attended = attend(labels, sources, q_norm, k_norm, values, got, whole, n_ctx, partners.shape[2])
     partial_out = jnp.dot(attended, out_weight, preferred_element_type=jnp.float32)
     mixed = lax.psum_scatter(
         partial_out.astype(jnp.bfloat16), "head", scatter_dimension=1, tiled=True

time: 549 us -> 460 us (0.84)
  local copies, waits for them, and re-layouts: 97.7 us -> 14 us
  Pallas kernels: 121 us -> 137 us
  matrix products: 14 us -> 5.19 us
  loops' own time: 8.29 us -> 0 us
    dynamic_slice x20 -> x2, local copies, waits for them, and re-layouts: 22.3 us -> 0.18 us  [shards(): sources = (partners[own_index] // blocks).reshape(-1)]
    while x26 -> x0, local copies, waits for them, and re-layouts: 21.3 us -> none  [the longest x2 18.6 us: shards(): attended = lax.map(one_block, jnp.arange(blocks)).reshape(tokens, width)]
    pallas_call x0 -> x1, Pallas kernels: none -> 15.8 us  [attend(): pl.pallas_call(attend_kernel, out_shape=jax.ShapeDtypeStruct((rows, width...]
    slice x1 -> x0, local copies, waits for them, and re-layouts: 9.63 us -> none  [shards(): got_blocks = got[:, :, :BLK]]
    gather x1 -> x0, local copies, waits for them, and re-layouts: 9.47 us -> none  [shards(): far = got_blocks[wanted // blocks]]
    dot_general x4 -> x0, matrix products: 8.83 us -> none  [the longest x2 5.76 us: attend_block(): jnp.einsum('qhd,khd->hqk', query_heads, key_heads, preferred_element_type...]
    another operation x1 -> x0, loops' own time: 8.29 us -> none  [shards(): attended = lax.map(one_block, jnp.arange(blocks)).reshape(tokens, width)]
    concatenate x6 -> x0, local copies, waits for them, and re-layouts: 7.8 us -> none  [attend_block(): key_set = jnp.concatenate([own_keys, far_keys, bank_keys], axis=0)]
where the time goes in v3:
time: 460 us; the launch traced here: 458 us
  waiting for transfers between devices  260 us (57%)
  Pallas kernels  137 us (30%)
  other arithmetic  19.8 us (4%)
  between operations  14.1 us (3%)
  local copies, waits for them, and re-layouts  14 us (3%)
  starting transfers between devices  8.32 us (2%)
  matrix products  5.19 us (1%)
    all_to_all x1, waiting for transfers between devices, shards(): got = lax.all_to_all(send, 'ctx', 0, 0, tiled=True)  196 us
    pallas_call x2, Pallas kernels, gather_all(): pl.pallas_call(functools.partial(gather_kernel, axis, other_axis, n), out...  121 us
    unnamed x2, waiting for transfers between devices  64.5 us
    pallas_call x1, Pallas kernels, attend(): pl.pallas_call(attend_kernel, out_shape=jax.ShapeDtypeStruct((rows, width...  15.8 us
    concatenate x1, other arithmetic, shards(): send = jnp.concatenate([send_blocks, send_bank], axis=2)  10.1 us
  transfers between devices with their start and end apart: 2, of which 2 were waited for; matrix products, arithmetic and copies ran while one was open for 0% of the time, Pallas kernels for 0%

profile of v3, /device:TPU:2, one launch (start us, length us, event | category | flops | bytes accessed | tf_op | source)
XLA Modules:
  0.0 458.4 jit_solution(11207590619345806507)
XLA Ops:
  7.2 0.8 fusion.6
  8.0 1.1 fusion
  9.1 1.1 fusion.3
  10.2 0.6 pad_maximum_fusion.2.piece_ref
  10.8 10.9 %shard_map.122 = f32[8,2,256]{2,1,0:T(2,128)} custom-call(f32[2,256]{1,0:T(2,128)} %pad_maximum_fusion.2.piece_ref), custom_call_target="tpu_custom_call" | custom-call | tf_op jit(solution)/shard_map/pallas_call | solution.py:61
  21.7 0.7 reduce_sum.40
  22.4 1.1 fusion.5.k_ref
  23.5 0.0 copy-start
  23.6 1.2 pad_maximum_fusion.1
  24.7 0.0 copy-start.1
  24.7 6.0 %gather_fusion = bf16[32,2,128,640]{3,2,1,0:T(8,128)(2,1)} fusion(bf16[2,2,128,640]{3,2,0,1:T(8,128)(2,1)S(1)} %pad_maximum_fusion.1, s32[1024]{0:T(1024)S(1)} %pad_clamp_fusion.1), kind=kCustom, calls=%fused_computation | custom fusion | bytes 20971648 | tf_op jit(solution)/shard_map/gather | solution.py:212
  30.8 0.0 copy-done
  30.8 1.6 maximum_bitcast_fusion
  32.4 10.1 %pad_maximum_fusion = bf16[32,2,160,640]{3,2,1,0:T(8,128)(2,1)} fusion(bf16[32,2,32,640]{3,2,1,0:T(8,128)(2,1)S(1)} %maximum_bitcast_fusion, bf16[32,2,128,640]{3,2,1,0:T(8,128)(2,1)} %gather_fusion), kind=kLoop, calls=%fused_computation.2 | loop fusion | flops 26214400 | bytes 26214400 | tf_op jit(solution)/shard_map/concatenate | solution.py:215
  42.5 8.3 %all-to-all-start = ((bf16[32,2,160,640]{3,2,1,0:T(8,128)(2,1)}), bf16[32,2,160,640]{3,2,1,0:T(8,128)(2,1)}, u32[]{:S(2)}, u32[]{:S(2)}) async-start(bf16[32,2,160,640]{3,2,1,0:T(8,128)(2,1)} %pad_maximum_fusion), calls=%async_computation | async-start | bytes 26214400 | tf_op jit(solution)/shard_map/all_to_all | solution.py:216
  50.8 0.0 reduce-scatter.4.cloned.1.call-start
  50.9 0.1 constant_dynamic-slice_fusion
  50.9 0.1 copy.14
  51.0 0.1 squeeze.3
  51.1 0.0 copy-done.5
  51.1 0.5 and_select_fusion.2.source_ref
  51.7 0.9 fusion.2.q_ref
  52.6 195.9 %all-to-all-done.got_ref = bf16[32,2,160,640]{3,2,1,0:T(8,128)(2,1)} async-done(((bf16[32,2,160,640]{3,2,1,0:T(8,128)(2,1)}), bf16[32,2,160,640]{3,2,1,0:T(8,128)(2,1)}, u32[]{:S(2)}, u32[]{:S(2)}) %all-to-all-start) | async-done | bytes 13107232 | tf_op jit(solution)/shard_map/all_to_all | solution.py:216
  248.4 2.0 slice.8
  250.4 1.2 gather_fusion.1
  251.7 110.0 %shard_map.123.whole_ref = bf16[32,128,640]{2,1,0:T(8,128)(2,1)} custom-call(bf16[128,640]{1,0:T(8,128)(2,1)} %bitcast.24), custom_call_target="tpu_custom_call" | custom-call | tf_op jit(solution)/shard_map/pallas_call | solution.py:61
  361.7 15.8 %shard_map.124 = bf16[256,640]{1,0:T(8,128)(2,1)} custom-call(s32[2]{0:T(128)} %label_ref.1, s32[24]{0:T(128)} %and_select_fusion.2.source_ref, bf16[256,640]{1,0:T(8,128)(2,1)} %fusion.2.q_ref, bf16[256,640]{1,0:T(8,128)(2,1)} %copy-done, bf16[256,640]{1,0:T(8,128)(2,1)} %v_ref.1, bf16[32,2,160,640]{3,2,1,0:T(8,128)(2,1)} %all-to-all-done.got_ref, ...), custom_call_target="tpu_custom_call" | custom-call | tf_op jit(solution)/shard_map/pallas_call | solution.py:131
  377.5 5.2 %convolution_convert_fusion = bf16[256,5120]{1,0:T(8,128)(2,1)S(1)} fusion(bf16[256,640]{1,0:T(8,128)(2,1)} %shard_map.124, bf16[640,5120]{1,0:T(8,128)(2,1)} %param.18), kind=kOutput, calls=%fused_computation.3 | convolution fusion | flops 1679032320 | bytes 9502720 | tf_op jit(solution)/shard_map/dot_general | solution.py:223
  382.7 2.6 copy.15
  385.3 0.0 reduce-scatter.4.cloned.1.call-update
  385.3 64.4 %reduce-scatter.4.cloned.1.call-done = bf16[640,256]{1,0:T(8,128)(2,1)} async-done(((bf16[5120,256]{1,0:T(8,128)(2,1)}), bf16[640,256]{1,0:T(8,128)(2,1)}) %reduce-scatter.4.cloned.1.call-update) | async-done | bytes 327696
  449.7 1.9 copy.16
  (13 shorter events, 0.1 us)
Async XLA Ops:
  23.5 7.2 %copy-start = (bf16[256,640]{1,0:T(8,128)(2,1)}, bf16[256,640]{1,0:T(8,128)(2,1)S(1)}, u32[]{:S(2)}) copy-start(bf16[256,640]{1,0:T(8,128)(2,1)S(1)} %fusion.5.k_ref) | copy-start | bytes 983044
  24.7 6.1 %copy-start.1 = (bf16[1024,640]{1,0:T(8,128)(2,1)S(1)}, bf16[1024,640]{1,0:T(8,128)(2,1)}, u32[]{:S(2)}) copy-start(bf16[1024,640]{1,0:T(8,128)(2,1)} %param.17) | copy-start | bytes 3932164
  42.5 8.4 %copy-start.3 = (s32[32,2,12]{0,1,2:T(2,128)S(1)}, s32[32,2,12]{0,1,2:T(2,128)}, u32[]{:S(2)}) copy-start(s32[32,2,12]{0,1,2:T(2,128)} %param.19) | copy-start | bytes 9220
  42.5 8.6 %copy-start.5 = (s32[2]{0:T(128)S(1)}, s32[2]{0:T(128)}, u32[]{:S(2)}) copy-start(s32[2]{0:T(128)} %param.20) | copy-start | bytes 28
  42.5 9.2 %copy-start.2 = (bf16[256,640]{1,0:T(8,128)(2,1)S(1)}, bf16[256,640]{1,0:T(8,128)(2,1)}, u32[]{:S(2)}) copy-start(bf16[256,640]{1,0:T(8,128)(2,1)} %param.11) | copy-start | bytes 983044
  42.5 9.2 %copy-start.4 = (f32[640]{0:T(1024)S(1)}, f32[640]{0:T(1024)}, u32[]{:S(2)}) copy-start(f32[640]{0:T(1024)} %param.14) | copy-start | bytes 7684
  42.5 205.9 %all-to-all-start = ((bf16[32,2,160,640]{3,2,1,0:T(8,128)(2,1)}), bf16[32,2,160,640]{3,2,1,0:T(8,128)(2,1)}, u32[]{:S(2)}, u32[]{:S(2)}) async-start(bf16[32,2,160,640]{3,2,1,0:T(8,128)(2,1)} %pad_maximum_fusion), calls=%async_computation | async-start | bytes 26214400 | tf_op jit(solution)/shard_map/all_to_all | solution.py:216
  50.8 398.9 %reduce-scatter.4.cloned.1.call-start = ((), (), s32[]{:S(2)}) async-start(), calls=%async_computation.2 | async-start | bytes 2949120
Sparse Core Ops, SparseCore 0:
  385.4 64.2 reduce-scatter.3

commit v4 on v3

--- a/solution.py
+++ b/solution.py
@@ -55,6 +55,75 @@
             device_id=device(source),
             device_id_type=MESH,
         ).wait_recv()
+
+
+def scatter_kernel(axis, other_axis, n, piece, keys_ref, values_ref, out_ref, send_sem, recv_sem, local_sem):
+    me = lax.axis_index(axis)
+    other = lax.axis_index(other_axis)
+
+    def device(j):
+        return (j, other) if axis == "ctx" else (other, j)
+
+    def rows(j):
+        return pl.ds(pl.multiple_of(j * piece, piece), piece)
+
+    barrier = pltpu.get_barrier_semaphore()
+    for k in range(1, n):
+        pl.semaphore_signal(barrier, inc=1, device_id=device(lax.rem(me + k, n)), device_id_type=MESH)
+    pl.semaphore_wait(barrier, n - 1)
+    sources = (keys_ref, values_ref)
+    local = [
+        pltpu.make_async_copy(src.at[rows(me)], out_ref.at[me, t], local_sem.at[t])
+        for t, src in enumerate(sources)
+    ]
+    for copy in local:
+        copy.start()
+    sends = []
+    for k in range(1, n):
+        peer = lax.rem(me + k, n)
+        for t, src in enumerate(sources):
+            copy = pltpu.make_async_remote_copy(
+                src_ref=src.at[rows(peer)],
+                dst_ref=out_ref.at[me, t],
+                send_sem=send_sem.at[k, t],
+                recv_sem=recv_sem.at[k, t],
+                device_id=device(peer),
+                device_id_type=MESH,
+            )
+            copy.start()
+            sends.append(copy)
+    for copy in local:
+        copy.wait()
+    for copy in sends:
+        copy.wait_send()
+    for k in range(1, n):
+        source = lax.rem(me + n - k, n)
+        for t, src in enumerate(sources):
+            pltpu.make_async_remote_copy(
+                src_ref=src.at[rows(me)],
+                dst_ref=out_ref.at[source, t],
+                send_sem=send_sem.at[k, t],
+                recv_sem=recv_sem.at[k, t],
+                device_id=device(source),
+                device_id_type=MESH,
+            ).wait_recv()
+
+
+def scatter_bank(ref_keys, ref_values, axis, other_axis, n, collective_id):
+    rows, width = ref_keys.shape
+    piece = rows // n
+    return pl.pallas_call(
+        functools.partial(scatter_kernel, axis, other_axis, n, piece),
+        out_shape=jax.ShapeDtypeStruct((n, 2, piece, width), ref_keys.dtype),
+        in_specs=[pl.BlockSpec(memory_space=pl.ANY)] * 2,
+        out_specs=pl.BlockSpec(memory_space=pl.ANY),
+        scratch_shapes=[
+            pltpu.SemaphoreType.DMA((n, 2)),
+            pltpu.SemaphoreType.DMA((n, 2)),
+            pltpu.SemaphoreType.DMA((2,)),
+        ],
+        compiler_params=pltpu.CompilerParams(collective_id=collective_id, has_side_effects=True),
+    )(ref_keys, ref_values)
 
 
 def gather_all(piece, axis, other_axis, n, collective_id):
@@ -209,12 +278,9 @@
     hit = (flat // blocks) == own_index
     pick = jnp.sum(jnp.where(hit, flat % blocks, 0), axis=1)
     kv_blocks = jnp.stack([key_blocks, value_blocks], axis=1)
-    send_blocks = kv_blocks[pick]
-    bank = jnp.stack([ref_keys, ref_values]).reshape(2, n_ctx, piece, width)
-    send_bank = jnp.transpose(bank, (1, 0, 2, 3))
-    send = jnp.concatenate([send_blocks, send_bank], axis=2)
+    send = kv_blocks[pick]
     got = lax.all_to_all(send, "ctx", 0, 0, tiled=True)
-    got_bank = got[:, :, BLK:]
+    got_bank = scatter_bank(ref_keys, ref_values, "ctx", "head", n_ctx, 3)
 
     sources = (partners[own_index] // blocks).reshape(-1)
     mine = got_bank[owners]

time: 460 us -> 438 us (0.952)
  waiting for transfers between devices: 260 us -> 49.9 us
  Pallas kernels: 137 us -> 338 us
  other arithmetic: 19.8 us -> 8.06 us
    all_to_all x1, waiting for transfers between devices: 196 us -> 0.01 us  [shards(): got = lax.all_to_all(send, 'ctx', 0, 0, tiled=True)]
    pallas_call x0 -> x1, Pallas kernels: none -> 193 us  [scatter_bank(): pl.pallas_call(functools.partial(scatter_kernel, axis, other_axis, n, pie...]
    unnamed x2, waiting for transfers between devices: 64.5 us -> 49.9 us
    concatenate x1 -> x0, other arithmetic: 10.1 us -> none  [shards(): send = jnp.concatenate([send_blocks, send_bank], axis=2)]
    pallas_call x2, Pallas kernels: 121 us -> 129 us  [gather_all(): pl.pallas_call(functools.partial(gather_kernel, axis, other_axis, n), out...]
  transfers between devices with their start and end apart: 2 -> 2, of which waited for: 2 -> 1; matrix products, arithmetic and copies ran while one was open for 0% -> 1% of each run, Pallas kernels for 0% -> 71%
where the time goes in v4:
time: 438 us; the launch traced here: 437 us
  Pallas kernels  338 us (77%)
  waiting for transfers between devices  49.9 us (11%)
  between operations  14.2 us (3%)
  local copies, waits for them, and re-layouts  13.4 us (3%)
  starting transfers between devices  8.5 us (2%)
  other arithmetic  8.06 us (2%)
  matrix products  5.19 us (1%)
    pallas_call x1, Pallas kernels, scatter_bank(): pl.pallas_call(functools.partial(scatter_kernel, axis, other_axis, n, pie...  193 us
    pallas_call x2, Pallas kernels, gather_all(): pl.pallas_call(functools.partial(gather_kernel, axis, other_axis, n), out...  129 us
    unnamed x2, waiting for transfers between devices  49.9 us
    pallas_call x1, Pallas kernels, attend(): pl.pallas_call(attend_kernel, out_shape=jax.ShapeDtypeStruct((rows, width...  15.7 us
  transfers between devices with their start and end apart: 2, of which 1 were waited for; matrix products, arithmetic and copies ran while one was open for 1% of the time, Pallas kernels for 71%

profile of v4, /device:TPU:2, one launch (start us, length us, event | category | flops | bytes accessed | tf_op | source)
XLA Modules:
  0.0 436.9 jit_solution(9618359875573810580)
XLA Ops:
  7.2 0.8 fusion.6
  8.0 1.1 fusion
  9.1 1.1 fusion.3
  10.2 0.6 pad_maximum_fusion.1.piece_ref
  10.8 10.9 %shard_map.122 = f32[8,2,256]{2,1,0:T(2,128)} custom-call(f32[2,256]{1,0:T(2,128)} %pad_maximum_fusion.1.piece_ref), custom_call_target="tpu_custom_call" | custom-call | tf_op jit(solution)/shard_map/pallas_call | solution.py:130
  21.7 0.7 reduce_sum.40
  22.4 1.1 fusion.5.k_ref
  23.5 0.0 copy-start
  23.6 1.2 pad_maximum_fusion
  24.7 5.7 %gather_fusion = bf16[32,2,128,640]{3,2,1,0:T(8,128)(2,1)} fusion(bf16[2,2,128,640]{3,2,0,1:T(8,128)(2,1)S(1)} %pad_maximum_fusion, s32[1024]{0:T(1024)S(1)} %pad_clamp_fusion.1), kind=kCustom, calls=%fused_computation | custom fusion | bytes 20971648 | tf_op jit(solution)/shard_map/gather | solution.py:281
  30.4 0.0 copy-done
  30.4 8.5 %all-to-all-start = ((bf16[32,2,128,640]{3,2,1,0:T(8,128)(2,1)}), bf16[32,2,128,640]{3,2,1,0:T(8,128)(2,1)}, u32[]{:S(2)}, u32[]{:S(2)}) async-start(bf16[32,2,128,640]{3,2,1,0:T(8,128)(2,1)} %gather_fusion), calls=%async_computation | async-start | bytes 20971520 | tf_op jit(solution)/shard_map/all_to_all | solution.py:282
  38.9 0.0 copy-start.1
  38.9 0.0 copy-start.3
  38.9 0.0 reduce-scatter.4.cloned.1.call-start
  39.0 0.0 copy-done.2
  39.0 0.1 constant_dynamic-slice_fusion
  39.1 0.1 copy.14
  39.2 0.1 squeeze.3
  39.3 192.6 %shard_map.123 = bf16[32,2,32,640]{3,2,1,0:T(8,128)(2,1)} custom-call(bf16[1024,640]{1,0:T(8,128)(2,1)} %keys_ref.1, bf16[1024,640]{1,0:T(8,128)(2,1)} %values_ref.1), custom_call_target="tpu_custom_call" | custom-call | tf_op jit(solution)/shard_map/pallas_call | solution.py:115
  231.9 3.0 gather_fusion.1
  234.9 118.5 %shard_map.124.whole_ref = bf16[32,128,640]{2,1,0:T(8,128)(2,1)} custom-call(bf16[128,640]{1,0:T(8,128)(2,1)} %bitcast.18), custom_call_target="tpu_custom_call" | custom-call | tf_op jit(solution)/shard_map/pallas_call | solution.py:130
  353.4 0.5 and_select_fusion.2.source_ref
  353.9 0.0 copy-done.1
  353.9 0.9 fusion.2.q_ref
  354.8 0.0 all-to-all-done.got_ref
  354.8 15.7 %shard_map.125 = bf16[256,640]{1,0:T(8,128)(2,1)} custom-call(s32[2]{0:T(128)} %label_ref.1, s32[24]{0:T(128)} %and_select_fusion.2.source_ref, bf16[256,640]{1,0:T(8,128)(2,1)} %fusion.2.q_ref, bf16[256,640]{1,0:T(8,128)(2,1)} %copy-done, bf16[256,640]{1,0:T(8,128)(2,1)} %v_ref.1, bf16[32,2,128,640]{3,2,1,0:T(8,128)(2,1)} %all-to-all-done.got_ref, ...), custom_call_target="tpu_custom_call" | custom-call | tf_op jit(solution)/shard_map/pallas_call | solution.py:200
  370.6 5.2 %convolution_convert_fusion = bf16[256,5120]{1,0:T(8,128)(2,1)S(1)} fusion(bf16[256,640]{1,0:T(8,128)(2,1)} %shard_map.125, bf16[640,5120]{1,0:T(8,128)(2,1)} %param.18), kind=kOutput, calls=%fused_computation.2 | convolution fusion | flops 1679032320 | bytes 9502720 | tf_op jit(solution)/shard_map/dot_general | solution.py:289
  375.8 2.6 copy.15
  378.3 0.0 reduce-scatter.4.cloned.1.call-update
  378.4 49.9 %reduce-scatter.4.cloned.1.call-done = bf16[640,256]{1,0:T(8,128)(2,1)} async-done(((bf16[5120,256]{1,0:T(8,128)(2,1)}), bf16[640,256]{1,0:T(8,128)(2,1)}) %reduce-scatter.4.cloned.1.call-update) | async-done | bytes 327696
  428.2 1.9 copy.16
  (9 shorter events, 0.0 us)
Async XLA Ops:
  23.5 6.9 %copy-start = (bf16[256,640]{1,0:T(8,128)(2,1)}, bf16[256,640]{1,0:T(8,128)(2,1)S(1)}, u32[]{:S(2)}) copy-start(bf16[256,640]{1,0:T(8,128)(2,1)S(1)} %fusion.5.k_ref) | copy-start | bytes 983044
  30.4 8.5 %copy-start.2 = (s32[32,2,12]{0,1,2:T(2,128)S(1)}, s32[32,2,12]{0,1,2:T(2,128)}, u32[]{:S(2)}) copy-start(s32[32,2,12]{0,1,2:T(2,128)} %param.19) | copy-start | bytes 9220
  30.4 201.4 %copy-start.4 = (s32[2]{0:T(128)S(1)}, s32[2]{0:T(128)}, u32[]{:S(2)}) copy-start(s32[2]{0:T(128)} %param.20) | copy-start | bytes 28
  30.4 324.4 %all-to-all-start = ((bf16[32,2,128,640]{3,2,1,0:T(8,128)(2,1)}), bf16[32,2,128,640]{3,2,1,0:T(8,128)(2,1)}, u32[]{:S(2)}, u32[]{:S(2)}) async-start(bf16[32,2,128,640]{3,2,1,0:T(8,128)(2,1)} %gather_fusion), calls=%async_computation | async-start | bytes 20971520 | tf_op jit(solution)/shard_map/all_to_all | solution.py:282
  38.9 315.0 %copy-start.1 = (bf16[256,640]{1,0:T(8,128)(2,1)S(1)}, bf16[256,640]{1,0:T(8,128)(2,1)}, u32[]{:S(2)}) copy-start(bf16[256,640]{1,0:T(8,128)(2,1)} %param.11) | copy-start | bytes 983044
  38.9 315.0 %copy-start.3 = (f32[640]{0:T(1024)S(1)}, f32[640]{0:T(1024)}, u32[]{:S(2)}) copy-start(f32[640]{0:T(1024)} %param.14) | copy-start | bytes 7684
  38.9 389.3 %reduce-scatter.4.cloned.1.call-start = ((), (), s32[]{:S(2)}) async-start(), calls=%async_computation.2 | async-start | bytes 2949120
Sparse Core Ops, SparseCore 0:
  378.5 49.6 reduce-scatter.3

commit v5 on v4

--- a/solution.py
+++ b/solution.py
@@ -142,7 +142,7 @@
 
 
 def attend_kernel(
-    label_ref, source_ref, q_ref, k_ref, v_ref, got_ref, whole_ref, o_ref,
+    label_ref, source_ref, q_ref, k_ref, v_ref, factor_ref, gain_ref, got_ref, whole_ref, o_ref,
     far_k, far_v, bank_k, bank_v, sem_k, sem_v, sem_bank,
 ):
     position = pl.program_id(0)
@@ -164,6 +164,7 @@
         copy.start()
     for copy in copies:
         copy.wait()
+    far_k[...] = (far_k[...].astype(jnp.float32) * factor_ref[...] * gain_ref[...]).astype(far_k.dtype)
     rows, width = q_ref.shape
     bank_rows = bank_k.shape[0] * piece
     dims = (((1,), (1,)), ((), ()))
@@ -193,7 +194,7 @@
         o_ref[:, cols] = (summed / total).astype(o_ref.dtype)
 
 
-def attend(labels, sources, q_norm, k_norm, values, got, whole, n_ctx, far_count):
+def attend(labels, sources, q_norm, k_norm, values, far_factor, k_gain, got, whole, n_ctx, far_count):
     rows, width = q_norm.shape
     piece = whole.shape[1] // 4
     block = pl.BlockSpec((BLK, width), lambda b, lab, src: (b, 0))
@@ -203,7 +204,15 @@
         grid_spec=pltpu.PrefetchScalarGridSpec(
             num_scalar_prefetch=2,
             grid=(rows // BLK,),
-            in_specs=[block, block, block, pl.BlockSpec(memory_space=pl.ANY), pl.BlockSpec(memory_space=pl.ANY)],
+            in_specs=[
+                block,
+                block,
+                block,
+                pl.BlockSpec((None, far_count * BLK, 1), lambda b, lab, src: (lab[b], 0, 0)),
+                pl.BlockSpec((1, width), lambda b, lab, src: (0, 0)),
+                pl.BlockSpec(memory_space=pl.ANY),
+                pl.BlockSpec(memory_space=pl.ANY),
+            ],
             out_specs=block,
             scratch_shapes=[
                 pltpu.VMEM((far_count * BLK, width), jnp.bfloat16),
@@ -216,7 +225,7 @@
             ],
         ),
         compiler_params=pltpu.CompilerParams(dimension_semantics=("arbitrary",)),
-    )(labels, sources, q_norm, k_norm, values, got, whole)
+    )(labels, sources, q_norm, k_norm, values, far_factor, k_gain.reshape(1, width), got, whole)
 
 
 def normalize(features, scale_gain, square_total):
@@ -269,9 +278,10 @@
     squares = jnp.stack([jnp.sum(q_float * q_float, axis=1), jnp.sum(k_float * k_float, axis=1)])
     q_total, k_total = jnp.sum(gather_all(squares, "head", "ctx", n_head, 1), axis=0)
     q_norm = normalize(q_float, q_gain, q_total)
-    k_norm = normalize(k_float, k_gain, k_total)
+    k_factor = lax.rsqrt(k_total / D + epsilon)
+    k_norm = (k_float * k_factor[:, None] * k_gain[None, :]).astype(jnp.bfloat16)
     query_blocks = q_norm.reshape(blocks, BLK, width)
-    key_blocks = k_norm.reshape(blocks, BLK, width)
+    key_blocks = keys.reshape(blocks, BLK, width)
     value_blocks = values.reshape(blocks, BLK, width)
 
     flat = partners.reshape(n_ctx, -1)
@@ -283,9 +293,14 @@
     got_bank = scatter_bank(ref_keys, ref_values, "ctx", "head", n_ctx, 3)
 
     sources = (partners[own_index] // blocks).reshape(-1)
+    factor_all = gather_all(k_factor.reshape(blocks, BLK), "ctx", "head", n_ctx, 4)
+    far_factor = factor_all[partners[own_index] // blocks, partners[own_index] % blocks]
+    far_factor = far_factor.reshape(persons, -1, 1)
     mine = got_bank[owners]
     whole = gather_all(mine.reshape(-1, width), "ctx", "head", n_ctx, 2)
-    attended = attend(labels, sources, q_norm, k_norm, values, got, whole, n_ctx, partners.shape[2])
+    attended = attend(
+        labels, sources, q_norm, k_norm, values, far_factor, k_gain, got, whole, n_ctx, partners.shape[2]
+    )
     partial_out = jnp.dot(attended, out_weight, preferred_element_type=jnp.float32)
     mixed = lax.psum_scatter(
         partial_out.astype(jnp.bfloat16), "head", scatter_dimension=1, tiled=True

time: 438 us -> 454 us (1.037)
  Pallas kernels: 338 us -> 348 us
  local copies, waits for them, and re-layouts: 13.4 us -> 18.4 us
    pallas_call x2 -> x3, Pallas kernels: 129 us -> 281 us  [gather_all(): pl.pallas_call(functools.partial(gather_kernel, axis, other_axis, n), out...]
    pallas_call x1, Pallas kernels: 193 us -> 49.9 us  [scatter_bank(): pl.pallas_call(functools.partial(scatter_kernel, axis, other_axis, n, pie...]
  transfers between devices with their start and end apart: 2 -> 2, of which waited for: 1 -> 1; matrix products, arithmetic and copies ran while one was open for 1% -> 3% of each run, Pallas kernels for 71% -> 73%
where the time goes in v5:
time: 454 us; the launch traced here: 452 us
  Pallas kernels  348 us (77%)
  waiting for transfers between devices  51.9 us (11%)
  local copies, waits for them, and re-layouts  18.4 us (4%)
  between operations  14.2 us (3%)
  starting transfers between devices  9.22 us (2%)
  other arithmetic  5.78 us (1%)
  matrix products  5.19 us (1%)
    pallas_call x3, Pallas kernels, gather_all(): pl.pallas_call(functools.partial(gather_kernel, axis, other_axis, n), out...  281 us
    unnamed x2, waiting for transfers between devices  51.9 us
    pallas_call x1, Pallas kernels, scatter_bank(): pl.pallas_call(functools.partial(scatter_kernel, axis, other_axis, n, pie...  49.9 us
    pallas_call x1, Pallas kernels, attend(): pl.pallas_call(attend_kernel, out_shape=jax.ShapeDtypeStruct((rows, width...  17.2 us
    all_to_all x1, starting transfers between devices, shards(): got = lax.all_to_all(send, 'ctx', 0, 0, tiled=True)  9.18 us
  transfers between devices with their start and end apart: 2, of which 1 were waited for; matrix products, arithmetic and copies ran while one was open for 3% of the time, Pallas kernels for 73%

profile of v5, /device:TPU:2, one launch (start us, length us, event | category | flops | bytes accessed | tf_op | source)
XLA Modules:
  0.0 452.2 jit_solution(18379929395499931582)
XLA Ops:
  7.2 0.8 fusion.6
  8.0 1.1 pad_maximum_fusion
  9.1 5.9 %gather_fusion.1 = bf16[32,2,128,640]{3,2,1,0:T(8,128)(2,1)} fusion(bf16[2,2,128,640]{3,2,0,1:T(8,128)(2,1)S(1)} %pad_maximum_fusion, s32[1024]{0:T(1024)S(1)} %pad_clamp_fusion.1), kind=kCustom, calls=%fused_computation.1 | custom fusion | bytes 20971648 | tf_op jit(solution)/shard_map/gather | solution.py:291
  15.0 9.2 %all-to-all-start = ((bf16[32,2,128,640]{3,2,1,0:T(8,128)(2,1)}), bf16[32,2,128,640]{3,2,1,0:T(8,128)(2,1)}, u32[]{:S(2)}, u32[]{:S(2)}) async-start(bf16[32,2,128,640]{3,2,1,0:T(8,128)(2,1)} %gather_fusion.1), calls=%async_computation | async-start | bytes 20971520 | tf_op jit(solution)/shard_map/all_to_all | solution.py:292
  24.2 0.0 copy-start.6
  24.2 0.0 reduce-scatter.4.cloned.1.call-start
  24.3 0.1 constant_dynamic-slice_fusion
  24.4 0.1 copy.18
  24.5 0.1 squeeze.7
  24.6 0.1 reshape.182
  24.7 0.1 fusion.3
  24.8 0.1 fusion
  25.0 0.6 pad_maximum_fusion.1.piece_ref
  25.6 162.3 %shard_map.122 = f32[8,2,256]{2,1,0:T(2,128)} custom-call(f32[2,256]{1,0:T(2,128)} %pad_maximum_fusion.1.piece_ref), custom_call_target="tpu_custom_call" | custom-call | tf_op jit(solution)/shard_map/pallas_call | solution.py:130
  187.9 0.7 reduce_sum.40
  188.6 0.6 fusion.11
  189.2 20.1 %shard_map.123 = f32[32,2,128]{2,1,0:T(2,128)} custom-call(f32[2,128]{1,0:T(2,128)} %bitcast.37), custom_call_target="tpu_custom_call" | custom-call | tf_op jit(solution)/shard_map/pallas_call | solution.py:130
  209.3 1.5 gather_fusion
  210.8 2.6 reshape.206.factor_ref
  213.4 49.9 %shard_map.124 = bf16[32,2,32,640]{3,2,1,0:T(8,128)(2,1)} custom-call(bf16[1024,640]{1,0:T(8,128)(2,1)} %keys_ref.1, bf16[1024,640]{1,0:T(8,128)(2,1)} %values_ref.1), custom_call_target="tpu_custom_call" | custom-call | tf_op jit(solution)/shard_map/pallas_call | solution.py:115
  263.3 3.0 gather_fusion.2
  266.3 98.1 %shard_map.125.whole_ref = bf16[32,128,640]{2,1,0:T(8,128)(2,1)} custom-call(bf16[128,640]{1,0:T(8,128)(2,1)} %bitcast.35), custom_call_target="tpu_custom_call" | custom-call | tf_op jit(solution)/shard_map/pallas_call | solution.py:130
  364.4 0.6 broadcast_in_dim.6.gain_ref
  365.0 0.6 and_select_fusion.4.source_ref
  365.6 1.1 fusion.2
  366.6 0.0 all-to-all-done.got_ref
  366.6 17.2 %shard_map.126 = bf16[256,640]{1,0:T(8,128)(2,1)} custom-call(s32[2]{0:T(128)} %label_ref.1, s32[24]{0:T(128)} %and_select_fusion.4.source_ref, bf16[256,640]{1,0:T(8,128)(2,1)} %get-tuple-element.4.q_ref, bf16[256,640]{1,0:T(8,128)(2,1)} %get-tuple-element.5.k_ref, bf16[256,640]{1,0:T(8,128)(2,1)} %v_ref.1, f32[2,1536,1]{2,1,0:T(8,128)} %reshape.206.factor_ref, ...), custom_call_target="tpu_custom_call" | custom-call | tf_op jit(solution)/shard_map/pallas_call | solution.py:201
  383.8 5.2 %convolution_convert_fusion = bf16[256,5120]{1,0:T(8,128)(2,1)S(1)} fusion(bf16[256,640]{1,0:T(8,128)(2,1)} %shard_map.126, bf16[640,5120]{1,0:T(8,128)(2,1)} %param.18), kind=kOutput, calls=%fused_computation.3 | convolution fusion | flops 1679032320 | bytes 9502720 | tf_op jit(solution)/shard_map/dot_general | solution.py:304
  389.0 2.6 copy.21
  391.6 0.0 reduce-scatter.4.cloned.1.call-update
  391.6 51.8 %reduce-scatter.4.cloned.1.call-done = bf16[640,256]{1,0:T(8,128)(2,1)} async-done(((bf16[5120,256]{1,0:T(8,128)(2,1)}), bf16[640,256]{1,0:T(8,128)(2,1)}) %reduce-scatter.4.cloned.1.call-update) | async-done | bytes 327696
  443.5 1.9 copy.22
  (18 shorter events, 0.1 us)
Async XLA Ops:
  15.0 9.3 %copy-start.2 = (s32[32,2,12]{0,1,2:T(2,128)S(1)}, s32[32,2,12]{0,1,2:T(2,128)}, u32[]{:S(2)}) copy-start(s32[32,2,12]{0,1,2:T(2,128)} %param.19) | copy-start | bytes 9220
  15.0 9.6 %copy-start = (bf16[256,640]{1,0:T(8,128)(2,1)S(1)}, bf16[256,640]{1,0:T(8,128)(2,1)}, u32[]{:S(2)}) copy-start(bf16[256,640]{1,0:T(8,128)(2,1)} %param.12) | copy-start | bytes 983044
  15.0 9.8 %copy-start.1 = (bf16[256,640]{1,0:T(8,128)(2,1)S(1)}, bf16[256,640]{1,0:T(8,128)(2,1)}, u32[]{:S(2)}) copy-start(bf16[256,640]{1,0:T(8,128)(2,1)} %param.11) | copy-start | bytes 983044
  15.0 351.6 %all-to-all-start = ((bf16[32,2,128,640]{3,2,1,0:T(8,128)(2,1)}), bf16[32,2,128,640]{3,2,1,0:T(8,128)(2,1)}, u32[]{:S(2)}, u32[]{:S(2)}) async-start(bf16[32,2,128,640]{3,2,1,0:T(8,128)(2,1)} %gather_fusion.1), calls=%async_computation | async-start | bytes 20971520 | tf_op jit(solution)/shard_map/all_to_all | solution.py:292
  24.2 239.1 %copy-start.6 = (s32[2]{0:T(128)S(1)}, s32[2]{0:T(128)}, u32[]{:S(2)}) copy-start(s32[2]{0:T(128)} %param.20) | copy-start | bytes 28
  24.2 419.2 %reduce-scatter.4.cloned.1.call-start = ((), (), s32[]{:S(2)}) async-start(), calls=%async_computation.2 | async-start | bytes 2949120
  213.4 151.0 %copy-start.3 = (f32[640]{0:T(1024)S(1)}, f32[640]{0:T(1024)}, u32[]{:S(2)}) copy-start(f32[640]{0:T(1024)} %param.15) | copy-start | bytes 7684
  213.4 152.2 %copy-start.4 = (f32[1,256]{1,0:T(1,128)S(1)}, f32[1,256]{1,0:T(1,128)}, u32[]{:S(2)}) copy-start(f32[1,256]{1,0:T(1,128)} %get-tuple-element.2) | copy-start | bytes 3076
  213.4 152.2 %copy-start.5 = (f32[640]{0:T(1024)S(1)}, f32[640]{0:T(1024)}, u32[]{:S(2)}) copy-start(f32[640]{0:T(1024)} %param.14) | copy-start | bytes 7684
Sparse Core Ops, SparseCore 0:
  391.7 51.6 reduce-scatter.3

commit v6 on v4

--- a/solution.py
+++ b/solution.py
@@ -284,7 +284,10 @@
 
     sources = (partners[own_index] // blocks).reshape(-1)
     mine = got_bank[owners]
-    whole = gather_all(mine.reshape(-1, width), "ctx", "head", n_ctx, 2)
+    piece_rows = mine.reshape(-1, width)
+    whole = lax.all_to_all(
+        jnp.broadcast_to(piece_rows, (n_ctx,) + piece_rows.shape), "ctx", 0, 0, tiled=True
+    )
     attended = attend(labels, sources, q_norm, k_norm, values, got, whole, n_ctx, partners.shape[2])
     partial_out = jnp.dot(attended, out_weight, preferred_element_type=jnp.float32)
     mixed = lax.psum_scatter(

time: 438 us -> 417 us (0.952)
  Pallas kernels: 338 us -> 135 us
  waiting for transfers between devices: 49.9 us -> 216 us
  starting transfers between devices: 8.5 us -> 26.4 us
    all_to_all x1, waiting for transfers between devices: 0.01 us -> 154 us  [shards(): got = lax.all_to_all(send, 'ctx', 0, 0, tiled=True)]
    pallas_call x1, Pallas kernels: 193 us -> 51.9 us  [scatter_bank(): pl.pallas_call(functools.partial(scatter_kernel, axis, other_axis, n, pie...]
    pallas_call x2 -> x1, Pallas kernels: 129 us -> 67.3 us  [gather_all(): pl.pallas_call(functools.partial(gather_kernel, axis, other_axis, n), out...]
    unnamed x2, waiting for transfers between devices: 49.9 us -> 61.9 us
    all_to_all x1, starting transfers between devices: 8.46 us -> 18.3 us  [shards(): got = lax.all_to_all(send, 'ctx', 0, 0, tiled=True)]
    all_to_all x0 -> x1, starting transfers between devices: none -> 8.05 us  [shards(): lax.all_to_all(jnp.broadcast_to(piece_rows, (n_ctx,) + piece_rows.shape),...]
  transfers between devices with their start and end apart: 2 -> 3, of which waited for: 1 -> 2; matrix products, arithmetic and copies ran while one was open for 1% -> 2% of each run, Pallas kernels for 71% -> 16%
where the time goes in v6:
time: 417 us
  waiting for transfers between devices  216 us (52%)
  Pallas kernels  135 us (32%)
  starting transfers between devices  26.4 us (6%)
  local copies, waits for them, and re-layouts  15.9 us (4%)
  between operations  14.2 us (3%)
  matrix products  5.19 us (1%)
    all_to_all x1, waiting for transfers between devices, shards(): got = lax.all_to_all(send, 'ctx', 0, 0, tiled=True)  154 us
    pallas_call x1, Pallas kernels, gather_all(): pl.pallas_call(functools.partial(gather_kernel, axis, other_axis, n), out...  67.3 us
    unnamed x2, waiting for transfers between devices  61.9 us
    pallas_call x1, Pallas kernels, scatter_bank(): pl.pallas_call(functools.partial(scatter_kernel, axis, other_axis, n, pie...  51.9 us
    all_to_all x1, starting transfers between devices, shards(): got = lax.all_to_all(send, 'ctx', 0, 0, tiled=True)  18.3 us
    pallas_call x1, Pallas kernels, attend(): pl.pallas_call(attend_kernel, out_shape=jax.ShapeDtypeStruct((rows, width...  15.8 us
  transfers between devices with their start and end apart: 3, of which 2 were waited for; matrix products, arithmetic and copies ran while one was open for 2% of the time, Pallas kernels for 16%

profile of v6, /device:TPU:2, one launch (start us, length us, event | category | flops | bytes accessed | tf_op | source)
XLA Modules:
  0.0 416.6 jit_solution(6853866807528510737)
XLA Ops:
  7.2 0.7 compare_select_fusion.1
  7.8 51.9 %shard_map.123 = bf16[32,2,32,640]{3,2,1,0:T(8,128)(2,1)} custom-call(bf16[1024,640]{1,0:T(8,128)(2,1)} %keys_ref.1, bf16[1024,640]{1,0:T(8,128)(2,1)} %values_ref.1), custom_call_target="tpu_custom_call" | custom-call | tf_op jit(solution)/shard_map/pallas_call | solution.py:115
  59.7 2.3 gather_fusion.1
  62.0 3.0 broadcast_in_dim.7
  65.1 0.0 copy-start.3
  65.1 8.0 %all-to-all-start.1 = ((bf16[32,128,640]{2,1,0:T(8,128)(2,1)}), bf16[32,128,640]{2,1,0:T(8,128)(2,1)}, u32[]{:S(2)}, u32[]{:S(2)}) async-start(bf16[32,128,640]{2,1,0:T(8,128)(2,1)} %broadcast_in_dim.7), calls=%async_computation.1 | async-start | bytes 10485760 | tf_op jit(solution)/shard_map/all_to_all | solution.py:288
  73.1 0.0 copy-done.2
  73.1 0.1 fusion
  73.3 0.1 fusion.3
  73.4 0.6 pad_maximum_fusion.1.piece_ref
  74.0 67.3 %shard_map.122 = f32[8,2,256]{2,1,0:T(2,128)} custom-call(f32[2,256]{1,0:T(2,128)} %pad_maximum_fusion.1.piece_ref), custom_call_target="tpu_custom_call" | custom-call | tf_op jit(solution)/shard_map/pallas_call | solution.py:130
  141.3 0.7 reduce_sum.40
  142.1 0.1 fusion.6
  142.2 0.1 fusion.5.k_ref
  142.4 0.1 pad_maximum_fusion
  142.4 5.8 %gather_fusion = bf16[32,2,128,640]{3,2,1,0:T(8,128)(2,1)} fusion(bf16[2,2,128,640]{3,2,0,1:T(8,128)(2,1)S(1)} %pad_maximum_fusion, s32[1024]{0:T(1024)S(1)} %pad_clamp_fusion.1), kind=kCustom, calls=%fused_computation | custom fusion | bytes 20971648 | tf_op jit(solution)/shard_map/gather | solution.py:281
  148.2 0.0 all-to-all-done.1.whole_ref
  148.3 18.3 %all-to-all-start = ((bf16[32,2,128,640]{3,2,1,0:T(8,128)(2,1)}), bf16[32,2,128,640]{3,2,1,0:T(8,128)(2,1)}, u32[]{:S(2)}, u32[]{:S(2)}) async-start(bf16[32,2,128,640]{3,2,1,0:T(8,128)(2,1)} %gather_fusion), calls=%async_computation | async-start | bytes 20971520 | tf_op jit(solution)/shard_map/all_to_all | solution.py:282
  166.6 0.0 reduce-scatter.4.cloned.1.call-start
  166.6 0.1 constant_dynamic-slice_fusion
  166.7 0.1 copy.14
  166.8 0.1 squeeze.3
  166.9 0.6 and_select_fusion.2.source_ref
  167.5 0.0 copy-done.6
  167.5 0.9 fusion.2.q_ref
  168.4 154.2 %all-to-all-done.got_ref = bf16[32,2,128,640]{3,2,1,0:T(8,128)(2,1)} async-done(((bf16[32,2,128,640]{3,2,1,0:T(8,128)(2,1)}), bf16[32,2,128,640]{3,2,1,0:T(8,128)(2,1)}, u32[]{:S(2)}, u32[]{:S(2)}) %all-to-all-start) | async-done | bytes 10485792 | tf_op jit(solution)/shard_map/all_to_all | solution.py:282
  322.5 15.8 %shard_map.124 = bf16[256,640]{1,0:T(8,128)(2,1)} custom-call(s32[2]{0:T(128)} %label_ref.1, s32[24]{0:T(128)} %and_select_fusion.2.source_ref, bf16[256,640]{1,0:T(8,128)(2,1)} %fusion.2.q_ref, bf16[256,640]{1,0:T(8,128)(2,1)} %copy-done, bf16[256,640]{1,0:T(8,128)(2,1)} %v_ref.1, bf16[32,2,128,640]{3,2,1,0:T(8,128)(2,1)} %all-to-all-done.got_ref, ...), custom_call_target="tpu_custom_call" | custom-call | tf_op jit(solution)/shard_map/pallas_call | solution.py:200
  338.3 5.2 %convolution_convert_fusion = bf16[256,5120]{1,0:T(8,128)(2,1)S(1)} fusion(bf16[256,640]{1,0:T(8,128)(2,1)} %shard_map.124, bf16[640,5120]{1,0:T(8,128)(2,1)} %param.18), kind=kOutput, calls=%fused_computation.2 | convolution fusion | flops 1679032320 | bytes 9502720 | tf_op jit(solution)/shard_map/dot_general | solution.py:292
  343.5 2.6 copy.15
  346.1 0.0 reduce-scatter.4.cloned.1.call-update
  346.1 61.8 %reduce-scatter.4.cloned.1.call-done = bf16[640,256]{1,0:T(8,128)(2,1)} async-done(((bf16[5120,256]{1,0:T(8,128)(2,1)}), bf16[640,256]{1,0:T(8,128)(2,1)}) %reduce-scatter.4.cloned.1.call-update) | async-done | bytes 327696
  407.9 1.9 copy.16
  (15 shorter events, 0.1 us)
Async XLA Ops:
  65.0 8.1 %copy-start.2 = (bf16[256,640]{1,0:T(8,128)(2,1)S(1)}, bf16[256,640]{1,0:T(8,128)(2,1)}, u32[]{:S(2)}) copy-start(bf16[256,640]{1,0:T(8,128)(2,1)} %param.11) | copy-start | bytes 983044
  65.0 8.2 %copy-start.1 = (bf16[256,640]{1,0:T(8,128)(2,1)S(1)}, bf16[256,640]{1,0:T(8,128)(2,1)}, u32[]{:S(2)}) copy-start(bf16[256,640]{1,0:T(8,128)(2,1)} %param.12) | copy-start | bytes 983044
  65.0 77.0 %copy-start.4 = (s32[32,2,12]{0,1,2:T(2,128)S(1)}, s32[32,2,12]{0,1,2:T(2,128)}, u32[]{:S(2)}) copy-start(s32[32,2,12]{0,1,2:T(2,128)} %param.19) | copy-start | bytes 9220
  65.0 77.1 %copy-start.5 = (f32[640]{0:T(1024)S(1)}, f32[640]{0:T(1024)}, u32[]{:S(2)}) copy-start(f32[640]{0:T(1024)} %param.15) | copy-start | bytes 7684
  65.1 77.3 %copy-start.3 = (bf16[256,640]{1,0:T(8,128)(2,1)S(1)}, bf16[256,640]{1,0:T(8,128)(2,1)}, u32[]{:S(2)}) copy-start(bf16[256,640]{1,0:T(8,128)(2,1)} %v_ref.1) | copy-start | bytes 983044
  65.1 83.2 %all-to-all-start.1 = ((bf16[32,128,640]{2,1,0:T(8,128)(2,1)}), bf16[32,128,640]{2,1,0:T(8,128)(2,1)}, u32[]{:S(2)}, u32[]{:S(2)}) async-start(bf16[32,128,640]{2,1,0:T(8,128)(2,1)} %broadcast_in_dim.7), calls=%async_computation.1 | async-start | bytes 10485760 | tf_op jit(solution)/shard_map/all_to_all | solution.py:288
  142.3 5.9 %copy-start = (bf16[256,640]{1,0:T(8,128)(2,1)}, bf16[256,640]{1,0:T(8,128)(2,1)S(1)}, u32[]{:S(2)}) copy-start(bf16[256,640]{1,0:T(8,128)(2,1)S(1)} %fusion.5.k_ref) | copy-start | bytes 983044
  148.2 19.3 %copy-start.6 = (f32[640]{0:T(1024)S(1)}, f32[640]{0:T(1024)}, u32[]{:S(2)}) copy-start(f32[640]{0:T(1024)} %param.14) | copy-start | bytes 7684
  148.3 174.3 %all-to-all-start = ((bf16[32,2,128,640]{3,2,1,0:T(8,128)(2,1)}), bf16[32,2,128,640]{3,2,1,0:T(8,128)(2,1)}, u32[]{:S(2)}, u32[]{:S(2)}) async-start(bf16[32,2,128,640]{3,2,1,0:T(8,128)(2,1)} %gather_fusion), calls=%async_computation | async-start | bytes 20971520 | tf_op jit(solution)/shard_map/all_to_all | solution.py:282
  166.6 241.4 %reduce-scatter.4.cloned.1.call-start = ((), (), s32[]{:S(2)}) async-start(), calls=%async_computation.3 | async-start | bytes 2949120
Sparse Core Ops, SparseCore 0:
  346.2 61.6 reduce-scatter.3

commit v7 on v6

--- a/solution.py
+++ b/solution.py
@@ -278,9 +278,12 @@
     hit = (flat // blocks) == own_index
     pick = jnp.sum(jnp.where(hit, flat % blocks, 0), axis=1)
     kv_blocks = jnp.stack([key_blocks, value_blocks], axis=1)
-    send = kv_blocks[pick]
+    send_blocks = kv_blocks[pick]
+    bank = jnp.stack([ref_keys, ref_values]).reshape(2, n_ctx, piece, width)
+    send_bank = jnp.transpose(bank, (1, 0, 2, 3))
+    send = jnp.concatenate([send_blocks, send_bank], axis=2)
     got = lax.all_to_all(send, "ctx", 0, 0, tiled=True)
-    got_bank = scatter_bank(ref_keys, ref_values, "ctx", "head", n_ctx, 3)
+    got_bank = got[:, :, BLK:]
 
     sources = (partners[own_index] // blocks).reshape(-1)
     mine = got_bank[owners]

time: 417 us -> 433 us (1.038)
  Pallas kernels: 135 us -> 26.6 us
  waiting for transfers between devices: 216 us -> 316 us
  other arithmetic: 4.08 us -> 19.8 us
  starting transfers between devices: 26.4 us -> 33.6 us
    all_to_all x1, waiting for transfers between devices: 0.01 us -> 65.9 us  [shards(): lax.all_to_all(jnp.broadcast_to(piece_rows, (n_ctx,) + piece_rows.shape),...]
    pallas_call x1, Pallas kernels: 67.3 us -> 10.9 us  [gather_all(): pl.pallas_call(functools.partial(gather_kernel, axis, other_axis, n), out...]
    pallas_call x1 -> x0, Pallas kernels: 51.9 us -> none  [scatter_bank(): pl.pallas_call(functools.partial(scatter_kernel, axis, other_axis, n, pie...]
    all_to_all x1, waiting for transfers between devices: 154 us -> 198 us  [shards(): got = lax.all_to_all(send, 'ctx', 0, 0, tiled=True)]
    all_to_all x1, starting transfers between devices: 8.05 us -> 25.3 us  [shards(): lax.all_to_all(jnp.broadcast_to(piece_rows, (n_ctx,) + piece_rows.shape),...]
    concatenate x0 -> x1, other arithmetic: none -> 10.1 us  [shards(): send = jnp.concatenate([send_blocks, send_bank], axis=2)]
    all_to_all x1, starting transfers between devices: 18.3 us -> 8.24 us  [shards(): got = lax.all_to_all(send, 'ctx', 0, 0, tiled=True)]
    unnamed x2, waiting for transfers between devices: 61.9 us -> 52.8 us
  transfers between devices with their start and end apart: 3 -> 3, of which waited for: 2 -> 3; matrix products, arithmetic and copies ran while one was open for 2% -> 0% of each run, Pallas kernels for 16% -> 0%
where the time goes in v7:
time: 433 us; the launch traced here: 432 us
  waiting for transfers between devices  316 us (73%)
  starting transfers between devices  33.6 us (8%)
  Pallas kernels  26.6 us (6%)
  other arithmetic  19.8 us (5%)
  local copies, waits for them, and re-layouts  16.4 us (4%)
  between operations  14.2 us (3%)
  matrix products  5.19 us (1%)
    all_to_all x1, waiting for transfers between devices, shards(): got = lax.all_to_all(send, 'ctx', 0, 0, tiled=True)  198 us
    all_to_all x1, waiting for transfers between devices, shards(): lax.all_to_all(jnp.broadcast_to(piece_rows, (n_ctx,) + piece_rows.shape),...  65.9 us
    unnamed x2, waiting for transfers between devices  52.8 us
    all_to_all x1, starting transfers between devices, shards(): lax.all_to_all(jnp.broadcast_to(piece_rows, (n_ctx,) + piece_rows.shape),...  25.3 us
    pallas_call x1, Pallas kernels, attend(): pl.pallas_call(attend_kernel, out_shape=jax.ShapeDtypeStruct((rows, width...  15.8 us
    pallas_call x1, Pallas kernels, gather_all(): pl.pallas_call(functools.partial(gather_kernel, axis, other_axis, n), out...  10.9 us
    concatenate x1, other arithmetic, shards(): send = jnp.concatenate([send_blocks, send_bank], axis=2)  10.1 us
  transfers between devices with their start and end apart: 3, of which 3 were waited for; matrix products, arithmetic and copies ran while one was open for 0% of the time, Pallas kernels for 0%

profile of v7, /device:TPU:2, one launch (start us, length us, event | category | flops | bytes accessed | tf_op | source)
XLA Modules:
  0.0 432.0 jit_solution(2888218145867524156)
XLA Ops:
  7.2 0.8 fusion.6
  8.0 1.1 fusion
  9.1 1.1 fusion.3
  10.2 0.6 pad_maximum_fusion.2.piece_ref
  10.8 10.9 %shard_map.122 = f32[8,2,256]{2,1,0:T(2,128)} custom-call(f32[2,256]{1,0:T(2,128)} %pad_maximum_fusion.2.piece_ref), custom_call_target="tpu_custom_call" | custom-call | tf_op jit(solution)/shard_map/pallas_call | solution.py:130
  21.7 0.7 reduce_sum.40
  22.4 1.1 fusion.5.k_ref
  23.5 0.0 copy-start
  23.6 1.2 pad_maximum_fusion.1
  24.7 0.0 copy-start.1
  24.7 6.0 %gather_fusion = bf16[32,2,128,640]{3,2,1,0:T(8,128)(2,1)} fusion(bf16[2,2,128,640]{3,2,0,1:T(8,128)(2,1)S(1)} %pad_maximum_fusion.1, s32[1024]{0:T(1024)S(1)} %pad_clamp_fusion.1), kind=kCustom, calls=%fused_computation | custom fusion | bytes 20971648 | tf_op jit(solution)/shard_map/gather | solution.py:281
  30.8 1.6 maximum_bitcast_fusion
  32.4 10.1 %pad_maximum_fusion = bf16[32,2,160,640]{3,2,1,0:T(8,128)(2,1)} fusion(bf16[32,2,32,640]{3,2,1,0:T(8,128)(2,1)S(1)} %maximum_bitcast_fusion, bf16[32,2,128,640]{3,2,1,0:T(8,128)(2,1)} %gather_fusion), kind=kLoop, calls=%fused_computation.2 | loop fusion | flops 26214400 | bytes 26214400 | tf_op jit(solution)/shard_map/concatenate | solution.py:284
  42.5 8.2 %all-to-all-start = ((bf16[32,2,160,640]{3,2,1,0:T(8,128)(2,1)}), bf16[32,2,160,640]{3,2,1,0:T(8,128)(2,1)}, u32[]{:S(2)}, u32[]{:S(2)}) async-start(bf16[32,2,160,640]{3,2,1,0:T(8,128)(2,1)} %pad_maximum_fusion), calls=%async_computation | async-start | bytes 26214400 | tf_op jit(solution)/shard_map/all_to_all | solution.py:285
  50.8 197.6 %all-to-all-done.got_ref = bf16[32,2,160,640]{3,2,1,0:T(8,128)(2,1)} async-done(((bf16[32,2,160,640]{3,2,1,0:T(8,128)(2,1)}), bf16[32,2,160,640]{3,2,1,0:T(8,128)(2,1)}, u32[]{:S(2)}, u32[]{:S(2)}) %all-to-all-start) | async-done | bytes 13107232 | tf_op jit(solution)/shard_map/all_to_all | solution.py:285
  248.4 2.0 slice.8
  250.4 0.6 gather_fusion.1
  251.0 3.0 broadcast_in_dim.7
  254.0 25.3 %all-to-all-start.1 = ((bf16[32,128,640]{2,1,0:T(8,128)(2,1)}), bf16[32,128,640]{2,1,0:T(8,128)(2,1)}, u32[]{:S(2)}, u32[]{:S(2)}) async-start(bf16[32,128,640]{2,1,0:T(8,128)(2,1)} %broadcast_in_dim.7), calls=%async_computation.1 | async-start | bytes 10485760 | tf_op jit(solution)/shard_map/all_to_all | solution.py:291
  279.3 0.0 reduce-scatter.4.cloned.1.call-start
  279.4 0.1 constant_dynamic-slice_fusion
  279.4 0.1 copy.14
  279.5 0.1 squeeze.3
  279.6 0.5 and_select_fusion.2.source_ref
  280.2 0.9 fusion.2.q_ref
  281.0 65.9 %all-to-all-done.1.whole_ref = bf16[32,128,640]{2,1,0:T(8,128)(2,1)} async-done(((bf16[32,128,640]{2,1,0:T(8,128)(2,1)}), bf16[32,128,640]{2,1,0:T(8,128)(2,1)}, u32[]{:S(2)}, u32[]{:S(2)}) %all-to-all-start.1) | async-done | bytes 5242912 | tf_op jit(solution)/shard_map/all_to_all | solution.py:291
  346.9 15.8 %shard_map.123 = bf16[256,640]{1,0:T(8,128)(2,1)} custom-call(s32[2]{0:T(128)} %label_ref.1, s32[24]{0:T(128)} %and_select_fusion.2.source_ref, bf16[256,640]{1,0:T(8,128)(2,1)} %fusion.2.q_ref, bf16[256,640]{1,0:T(8,128)(2,1)} %copy-done, bf16[256,640]{1,0:T(8,128)(2,1)} %v_ref.1, bf16[32,2,160,640]{3,2,1,0:T(8,128)(2,1)} %all-to-all-done.got_ref, ...), custom_call_target="tpu_custom_call" | custom-call | tf_op jit(solution)/shard_map/pallas_call | solution.py:200
  362.7 5.2 %convolution_convert_fusion = bf16[256,5120]{1,0:T(8,128)(2,1)S(1)} fusion(bf16[256,640]{1,0:T(8,128)(2,1)} %shard_map.123, bf16[640,5120]{1,0:T(8,128)(2,1)} %param.18), kind=kOutput, calls=%fused_computation.3 | convolution fusion | flops 1679032320 | bytes 9502720 | tf_op jit(solution)/shard_map/dot_general | solution.py:295
  367.9 2.6 copy.15
  370.5 0.0 reduce-scatter.4.cloned.1.call-update
  370.5 52.8 %reduce-scatter.4.cloned.1.call-done = bf16[640,256]{1,0:T(8,128)(2,1)} async-done(((bf16[5120,256]{1,0:T(8,128)(2,1)}), bf16[640,256]{1,0:T(8,128)(2,1)}) %reduce-scatter.4.cloned.1.call-update) | async-done | bytes 327696
  423.3 1.9 copy.16
  (15 shorter events, 0.1 us)
Async XLA Ops:
  23.5 7.2 %copy-start = (bf16[256,640]{1,0:T(8,128)(2,1)}, bf16[256,640]{1,0:T(8,128)(2,1)S(1)}, u32[]{:S(2)}) copy-start(bf16[256,640]{1,0:T(8,128)(2,1)S(1)} %fusion.5.k_ref) | copy-start | bytes 983044
  24.7 6.1 %copy-start.1 = (bf16[1024,640]{1,0:T(8,128)(2,1)S(1)}, bf16[1024,640]{1,0:T(8,128)(2,1)}, u32[]{:S(2)}) copy-start(bf16[1024,640]{1,0:T(8,128)(2,1)} %param.17) | copy-start | bytes 3932164
  42.5 8.3 %copy-start.5 = (s32[2]{0:T(128)S(1)}, s32[2]{0:T(128)}, u32[]{:S(2)}) copy-start(s32[2]{0:T(128)} %param.20) | copy-start | bytes 28
  42.5 205.9 %all-to-all-start = ((bf16[32,2,160,640]{3,2,1,0:T(8,128)(2,1)}), bf16[32,2,160,640]{3,2,1,0:T(8,128)(2,1)}, u32[]{:S(2)}, u32[]{:S(2)}) async-start(bf16[32,2,160,640]{3,2,1,0:T(8,128)(2,1)} %pad_maximum_fusion), calls=%async_computation | async-start | bytes 26214400 | tf_op jit(solution)/shard_map/all_to_all | solution.py:285
  254.0 25.4 %copy-start.3 = (s32[32,2,12]{0,1,2:T(2,128)S(1)}, s32[32,2,12]{0,1,2:T(2,128)}, u32[]{:S(2)}) copy-start(s32[32,2,12]{0,1,2:T(2,128)} %param.19) | copy-start | bytes 9220
  254.0 26.2 %copy-start.2 = (bf16[256,640]{1,0:T(8,128)(2,1)S(1)}, bf16[256,640]{1,0:T(8,128)(2,1)}, u32[]{:S(2)}) copy-start(bf16[256,640]{1,0:T(8,128)(2,1)} %param.11) | copy-start | bytes 983044
  254.0 26.2 %copy-start.4 = (f32[640]{0:T(1024)S(1)}, f32[640]{0:T(1024)}, u32[]{:S(2)}) copy-start(f32[640]{0:T(1024)} %param.14) | copy-start | bytes 7684
  254.0 92.9 %all-to-all-start.1 = ((bf16[32,128,640]{2,1,0:T(8,128)(2,1)}), bf16[32,128,640]{2,1,0:T(8,128)(2,1)}, u32[]{:S(2)}, u32[]{:S(2)}) async-start(bf16[32,128,640]{2,1,0:T(8,128)(2,1)} %broadcast_in_dim.7), calls=%async_computation.1 | async-start | bytes 10485760 | tf_op jit(solution)/shard_map/all_to_all | solution.py:291
  279.3 144.0 %reduce-scatter.4.cloned.1.call-start = ((), (), s32[]{:S(2)}) async-start(), calls=%async_computation.3 | async-start | bytes 2949120
Sparse Core Ops, SparseCore 0:
  370.6 52.6 reduce-scatter.3

commit v8 on v6

--- a/solution.py
+++ b/solution.py
@@ -280,7 +280,8 @@
     kv_blocks = jnp.stack([key_blocks, value_blocks], axis=1)
     send = kv_blocks[pick]
     got = lax.all_to_all(send, "ctx", 0, 0, tiled=True)
-    got_bank = scatter_bank(ref_keys, ref_values, "ctx", "head", n_ctx, 3)
+    bank = jnp.stack([ref_keys, ref_values]).reshape(2, n_ctx, piece, width)
+    got_bank = lax.all_to_all(jnp.transpose(bank, (1, 0, 2, 3)), "ctx", 0, 0, tiled=True)
 
     sources = (partners[own_index] // blocks).reshape(-1)
     mine = got_bank[owners]

time: 417 us -> 412 us (0.988)
  Pallas kernels: 135 us -> 87.7 us
  waiting for transfers between devices: 216 us -> 250 us
  starting transfers between devices: 26.4 us -> 33.7 us
    pallas_call x1 -> x0, Pallas kernels: 51.9 us -> none  [scatter_bank(): pl.pallas_call(functools.partial(scatter_kernel, axis, other_axis, n, pie...]
    all_to_all x0 -> x1, waiting for transfers between devices: none -> 32.8 us  [shards(): lax.all_to_all(jnp.transpose(bank, (1, 0, 2, 3)), 'ctx', 0, 0, tiled=True)]
    all_to_all x0 -> x1, starting transfers between devices: none -> 9.1 us  [shards(): lax.all_to_all(jnp.transpose(bank, (1, 0, 2, 3)), 'ctx', 0, 0, tiled=True)]
    pallas_call x1, Pallas kernels: 67.3 us -> 72 us  [gather_all(): pl.pallas_call(functools.partial(gather_kernel, axis, other_axis, n), out...]
  transfers between devices with their start and end apart: 3 -> 4, of which waited for: 2 -> 3; matrix products, arithmetic and copies ran while one was open for 2% -> 2% of each run, Pallas kernels for 16% -> 17%
where the time goes in v8:
time: 412 us
  waiting for transfers between devices  250 us (61%)
  Pallas kernels  87.7 us (21%)
  starting transfers between devices  33.7 us (8%)
  between operations  14.2 us (3%)
  local copies, waits for them, and re-layouts  14 us (3%)
  other arithmetic  6.86 us (2%)
  matrix products  5.19 us (1%)
    all_to_all x1, waiting for transfers between devices, shards(): got = lax.all_to_all(send, 'ctx', 0, 0, tiled=True)  154 us
    pallas_call x1, Pallas kernels, gather_all(): pl.pallas_call(functools.partial(gather_kernel, axis, other_axis, n), out...  72 us
    unnamed x2, waiting for transfers between devices  62.7 us
    all_to_all x1, waiting for transfers between devices, shards(): lax.all_to_all(jnp.transpose(bank, (1, 0, 2, 3)), 'ctx', 0, 0, tiled=True)  32.8 us
    all_to_all x1, starting transfers between devices, shards(): got = lax.all_to_all(send, 'ctx', 0, 0, tiled=True)  17.5 us
    pallas_call x1, Pallas kernels, attend(): pl.pallas_call(attend_kernel, out_shape=jax.ShapeDtypeStruct((rows, width...  15.7 us
    all_to_all x1, starting transfers between devices, shards(): lax.all_to_all(jnp.transpose(bank, (1, 0, 2, 3)), 'ctx', 0, 0, tiled=True)  9.1 us
  transfers between devices with their start and end apart: 4, of which 3 were waited for; matrix products, arithmetic and copies ran while one was open for 2% of the time, Pallas kernels for 17%

profile of v8, /device:TPU:2, one launch (start us, length us, event | category | flops | bytes accessed | tf_op | source)
XLA Modules:
  0.0 411.5 jit_solution(17439435579556253955)
XLA Ops:
  7.2 3.5 maximum_bitcast_fusion
  10.7 9.1 %all-to-all-start.1 = ((bf16[32,2,32,640]{3,2,1,0:T(8,128)(2,1)}), bf16[32,2,32,640]{3,2,1,0:T(8,128)(2,1)S(1)}, u32[]{:S(2)}, u32[]{:S(2)}) async-start(bf16[32,2,32,640]{3,2,1,0:T(8,128)(2,1)} %maximum_bitcast_fusion), calls=%async_computation.1 | async-start | bytes 5242880 | tf_op jit(solution)/shard_map/all_to_all | solution.py:284
  19.8 32.8 %all-to-all-done.1 = bf16[32,2,32,640]{3,2,1,0:T(8,128)(2,1)S(1)} async-done(((bf16[32,2,32,640]{3,2,1,0:T(8,128)(2,1)}), bf16[32,2,32,640]{3,2,1,0:T(8,128)(2,1)S(1)}, u32[]{:S(2)}, u32[]{:S(2)}) %all-to-all-start.1) | async-done | bytes 2621472 | tf_op jit(solution)/shard_map/all_to_all | solution.py:284
  52.6 0.6 gather_fusion.1
  53.2 3.0 broadcast_in_dim.7
  56.2 0.0 copy-start.3
  56.2 7.1 %all-to-all-start.2 = ((bf16[32,128,640]{2,1,0:T(8,128)(2,1)}), bf16[32,128,640]{2,1,0:T(8,128)(2,1)}, u32[]{:S(2)}, u32[]{:S(2)}) async-start(bf16[32,128,640]{2,1,0:T(8,128)(2,1)} %broadcast_in_dim.7), calls=%async_computation.2 | async-start | bytes 10485760 | tf_op jit(solution)/shard_map/all_to_all | solution.py:289
  63.3 0.0 copy-done.2
  63.3 0.1 fusion
  63.5 0.1 fusion.3
  63.6 0.6 pad_maximum_fusion.1.piece_ref
  64.2 72.0 %shard_map.122 = f32[8,2,256]{2,1,0:T(2,128)} custom-call(f32[2,256]{1,0:T(2,128)} %pad_maximum_fusion.1.piece_ref), custom_call_target="tpu_custom_call" | custom-call | tf_op jit(solution)/shard_map/pallas_call | solution.py:130
  136.2 0.7 reduce_sum.40
  136.9 0.1 fusion.6
  137.1 0.1 fusion.5.k_ref
  137.2 0.1 pad_maximum_fusion
  137.3 5.7 %gather_fusion = bf16[32,2,128,640]{3,2,1,0:T(8,128)(2,1)} fusion(bf16[2,2,128,640]{3,2,0,1:T(8,128)(2,1)S(1)} %pad_maximum_fusion, s32[1024]{0:T(1024)S(1)} %pad_clamp_fusion.1), kind=kCustom, calls=%fused_computation | custom fusion | bytes 20971648 | tf_op jit(solution)/shard_map/gather | solution.py:281
  143.0 0.0 all-to-all-done.2.whole_ref
  143.1 17.5 %all-to-all-start = ((bf16[32,2,128,640]{3,2,1,0:T(8,128)(2,1)}), bf16[32,2,128,640]{3,2,1,0:T(8,128)(2,1)}, u32[]{:S(2)}, u32[]{:S(2)}) async-start(bf16[32,2,128,640]{3,2,1,0:T(8,128)(2,1)} %gather_fusion), calls=%async_computation | async-start | bytes 20971520 | tf_op jit(solution)/shard_map/all_to_all | solution.py:282
  160.6 0.0 reduce-scatter.4.cloned.1.call-start
  160.6 0.1 constant_dynamic-slice_fusion
  160.7 0.1 copy.14
  160.8 0.1 squeeze.3
  160.9 0.6 and_select_fusion.2.source_ref
  161.5 0.9 fusion.2.q_ref
  162.3 154.2 %all-to-all-done.got_ref = bf16[32,2,128,640]{3,2,1,0:T(8,128)(2,1)} async-done(((bf16[32,2,128,640]{3,2,1,0:T(8,128)(2,1)}), bf16[32,2,128,640]{3,2,1,0:T(8,128)(2,1)}, u32[]{:S(2)}, u32[]{:S(2)}) %all-to-all-start) | async-done | bytes 10485792 | tf_op jit(solution)/shard_map/all_to_all | solution.py:282
  316.6 15.7 %shard_map.123 = bf16[256,640]{1,0:T(8,128)(2,1)} custom-call(s32[2]{0:T(128)} %label_ref.1, s32[24]{0:T(128)} %and_select_fusion.2.source_ref, bf16[256,640]{1,0:T(8,128)(2,1)} %fusion.2.q_ref, bf16[256,640]{1,0:T(8,128)(2,1)} %copy-done, bf16[256,640]{1,0:T(8,128)(2,1)} %v_ref.1, bf16[32,2,128,640]{3,2,1,0:T(8,128)(2,1)} %all-to-all-done.got_ref, ...), custom_call_target="tpu_custom_call" | custom-call | tf_op jit(solution)/shard_map/pallas_call | solution.py:200
  332.3 5.2 %convolution_convert_fusion = bf16[256,5120]{1,0:T(8,128)(2,1)S(1)} fusion(bf16[256,640]{1,0:T(8,128)(2,1)} %shard_map.123, bf16[640,5120]{1,0:T(8,128)(2,1)} %param.18), kind=kOutput, calls=%fused_computation.2 | convolution fusion | flops 1679032320 | bytes 9502720 | tf_op jit(solution)/shard_map/dot_general | solution.py:293
  337.5 2.6 copy.15
  340.1 0.0 reduce-scatter.4.cloned.1.call-update
  340.1 62.7 %reduce-scatter.4.cloned.1.call-done = bf16[640,256]{1,0:T(8,128)(2,1)} async-done(((bf16[5120,256]{1,0:T(8,128)(2,1)}), bf16[640,256]{1,0:T(8,128)(2,1)}) %reduce-scatter.4.cloned.1.call-update) | async-done | bytes 327696
  402.8 1.9 copy.16
  (19 shorter events, 0.1 us)
Async XLA Ops:
  10.7 9.1 %copy-start.7 = (s32[2]{0:T(128)S(1)}, s32[2]{0:T(128)}, u32[]{:S(2)}) copy-start(s32[2]{0:T(128)} %param.20) | copy-start | bytes 28
  10.7 42.0 %all-to-all-start.1 = ((bf16[32,2,32,640]{3,2,1,0:T(8,128)(2,1)}), bf16[32,2,32,640]{3,2,1,0:T(8,128)(2,1)S(1)}, u32[]{:S(2)}, u32[]{:S(2)}) async-start(bf16[32,2,32,640]{3,2,1,0:T(8,128)(2,1)} %maximum_bitcast_fusion), calls=%async_computation.1 | async-start | bytes 5242880 | tf_op jit(solution)/shard_map/all_to_all | solution.py:284
  56.2 7.1 %copy-start.2 = (bf16[256,640]{1,0:T(8,128)(2,1)S(1)}, bf16[256,640]{1,0:T(8,128)(2,1)}, u32[]{:S(2)}) copy-start(bf16[256,640]{1,0:T(8,128)(2,1)} %param.11) | copy-start | bytes 983044
  56.2 7.2 %copy-start.1 = (bf16[256,640]{1,0:T(8,128)(2,1)S(1)}, bf16[256,640]{1,0:T(8,128)(2,1)}, u32[]{:S(2)}) copy-start(bf16[256,640]{1,0:T(8,128)(2,1)} %param.12) | copy-start | bytes 983044
  56.2 80.7 %copy-start.4 = (s32[32,2,12]{0,1,2:T(2,128)S(1)}, s32[32,2,12]{0,1,2:T(2,128)}, u32[]{:S(2)}) copy-start(s32[32,2,12]{0,1,2:T(2,128)} %param.19) | copy-start | bytes 9220
  56.2 80.8 %copy-start.5 = (f32[640]{0:T(1024)S(1)}, f32[640]{0:T(1024)}, u32[]{:S(2)}) copy-start(f32[640]{0:T(1024)} %param.15) | copy-start | bytes 7684
  56.2 81.0 %copy-start.3 = (bf16[256,640]{1,0:T(8,128)(2,1)S(1)}, bf16[256,640]{1,0:T(8,128)(2,1)}, u32[]{:S(2)}) copy-start(bf16[256,640]{1,0:T(8,128)(2,1)} %v_ref.1) | copy-start | bytes 983044
  56.2 86.8 %all-to-all-start.2 = ((bf16[32,128,640]{2,1,0:T(8,128)(2,1)}), bf16[32,128,640]{2,1,0:T(8,128)(2,1)}, u32[]{:S(2)}, u32[]{:S(2)}) async-start(bf16[32,128,640]{2,1,0:T(8,128)(2,1)} %broadcast_in_dim.7), calls=%async_computation.2 | async-start | bytes 10485760 | tf_op jit(solution)/shard_map/all_to_all | solution.py:289
  137.2 5.8 %copy-start = (bf16[256,640]{1,0:T(8,128)(2,1)}, bf16[256,640]{1,0:T(8,128)(2,1)S(1)}, u32[]{:S(2)}) copy-start(bf16[256,640]{1,0:T(8,128)(2,1)S(1)} %fusion.5.k_ref) | copy-start | bytes 983044
  143.0 18.4 %copy-start.6 = (f32[640]{0:T(1024)S(1)}, f32[640]{0:T(1024)}, u32[]{:S(2)}) copy-start(f32[640]{0:T(1024)} %param.14) | copy-start | bytes 7684
  143.1 173.5 %all-to-all-start = ((bf16[32,2,128,640]{3,2,1,0:T(8,128)(2,1)}), bf16[32,2,128,640]{3,2,1,0:T(8,128)(2,1)}, u32[]{:S(2)}, u32[]{:S(2)}) async-start(bf16[32,2,128,640]{3,2,1,0:T(8,128)(2,1)} %gather_fusion), calls=%async_computation | async-start | bytes 20971520 | tf_op jit(solution)/shard_map/all_to_all | solution.py:282
  160.6 242.2 %reduce-scatter.4.cloned.1.call-start = ((), (), s32[]{:S(2)}) async-start(), calls=%async_computation.4 | async-start | bytes 2949120
Sparse Core Ops, SparseCore 0:
  340.2 62.5 reduce-scatter.3

commit v9 on v8

--- a/solution.py
+++ b/solution.py
@@ -145,77 +145,85 @@
     label_ref, source_ref, q_ref, k_ref, v_ref, got_ref, whole_ref, o_ref,
     far_k, far_v, bank_k, bank_v, sem_k, sem_v, sem_bank,
 ):
-    position = pl.program_id(0)
-    person = label_ref[position]
-    far_count = far_k.shape[0] // BLK
-    piece = bank_k.shape[1]
-    copies = []
-    for j in range(far_count):
-        source = source_ref[person * far_count + j]
+    n_blocks = far_k.shape[0]
+    far_count = far_k.shape[1] // BLK
+    piece = bank_k.shape[2]
+    pending = []
+    for position in range(n_blocks):
+        person = label_ref[position]
+        copies = []
+        for j in range(far_count):
+            source = source_ref[person * far_count + j]
+            copies.append(pltpu.make_async_copy(
+                got_ref.at[source, 0, pl.ds(0, BLK)], far_k.at[position, pl.ds(j * BLK, BLK)],
+                sem_k.at[position, j]))
+            copies.append(pltpu.make_async_copy(
+                got_ref.at[source, 1, pl.ds(0, BLK)], far_v.at[position, pl.ds(j * BLK, BLK)],
+                sem_v.at[position, j]))
         copies.append(pltpu.make_async_copy(
-            got_ref.at[source, 0, pl.ds(0, BLK)], far_k.at[pl.ds(j * BLK, BLK)], sem_k.at[j]))
+            whole_ref.at[:, pl.ds(person * 2 * piece, piece)], bank_k.at[position], sem_bank.at[position, 0]))
         copies.append(pltpu.make_async_copy(
-            got_ref.at[source, 1, pl.ds(0, BLK)], far_v.at[pl.ds(j * BLK, BLK)], sem_v.at[j]))
-    copies.append(pltpu.make_async_copy(
-        whole_ref.at[:, pl.ds(person * 2 * piece, piece)], bank_k, sem_bank.at[0]))
-    copies.append(pltpu.make_async_copy(
-        whole_ref.at[:, pl.ds(person * 2 * piece + piece, piece)], bank_v, sem_bank.at[1]))
-    for copy in copies:
-        copy.start()
-    for copy in copies:
-        copy.wait()
-    rows, width = q_ref.shape
-    bank_rows = bank_k.shape[0] * piece
+            whole_ref.at[:, pl.ds(person * 2 * piece + piece, piece)], bank_v.at[position],
+            sem_bank.at[position, 1]))
+        for copy in copies:
+            copy.start()
+        pending.append(copies)
+    width = q_ref.shape[1]
+    bank_rows = bank_k.shape[1] * piece
     dims = (((1,), (1,)), ((), ()))
-    for h in range(width // HD):
-        cols = pl.ds(h * HD, HD)
-        query = q_ref[:, cols]
-        parts = [
-            (k_ref[:, cols], v_ref[:, cols]),
-            (far_k[:, cols], far_v[:, cols]),
-            (bank_k[:, :, cols].reshape(bank_rows, HD), bank_v[:, :, cols].reshape(bank_rows, HD)),
-        ]
-        scores = [
-            lax.dot_general(query, key, dims, preferred_element_type=jnp.float32) * HD ** (-0.5)
-            for key, _ in parts
-        ]
-        peak = jnp.max(scores[0], axis=1, keepdims=True)
-        for score in scores[1:]:
-            peak = jnp.maximum(peak, jnp.max(score, axis=1, keepdims=True))
-        total = None
-        summed = None
-        for score, (_, value) in zip(scores, parts):
-            exponent = jnp.exp(score - peak)
-            part_sum = jnp.sum(exponent, axis=1, keepdims=True)
-            product = jnp.dot(exponent.astype(jnp.bfloat16), value, preferred_element_type=jnp.float32)
-            total = part_sum if total is None else total + part_sum
-            summed = product if summed is None else summed + product
-        o_ref[:, cols] = (summed / total).astype(o_ref.dtype)
+    for position in range(n_blocks):
+        for copy in pending[position]:
+            copy.wait()
+        rows = pl.ds(position * BLK, BLK)
+        for h in range(width // HD):
+            cols = pl.ds(h * HD, HD)
+            query = q_ref[rows, cols]
+            parts = [
+                (k_ref[rows, cols], v_ref[rows, cols]),
+                (far_k[position, :, cols], far_v[position, :, cols]),
+                (
+                    bank_k[position, :, :, cols].reshape(bank_rows, HD),
+                    bank_v[position, :, :, cols].reshape(bank_rows, HD),
+                ),
+            ]
+            scores = [
+                lax.dot_general(query, key, dims, preferred_element_type=jnp.float32) * HD ** (-0.5)
+                for key, _ in parts
+            ]
+            peak = jnp.max(scores[0], axis=1, keepdims=True)
+            for score in scores[1:]:
+                peak = jnp.maximum(peak, jnp.max(score, axis=1, keepdims=True))
+            total = None
+            summed = None
+            for score, (_, value) in zip(scores, parts):
+                exponent = jnp.exp(score - peak)
+                part_sum = jnp.sum(exponent, axis=1, keepdims=True)
+                product = jnp.dot(exponent.astype(jnp.bfloat16), value, preferred_element_type=jnp.float32)
+                total = part_sum if total is None else total + part_sum
+                summed = product if summed is None else summed + product
+            o_ref[rows, cols] = (summed / total).astype(o_ref.dtype)
 
 
 def attend(labels, sources, q_norm, k_norm, values, got, whole, n_ctx, far_count):
     rows, width = q_norm.shape
+    n_blocks = rows // BLK
     piece = whole.shape[1] // 4
-    block = pl.BlockSpec((BLK, width), lambda b, lab, src: (b, 0))
+    vmem = pl.BlockSpec(memory_space=pltpu.VMEM)
+    smem = pl.BlockSpec(memory_space=pltpu.SMEM)
     return pl.pallas_call(
         attend_kernel,
         out_shape=jax.ShapeDtypeStruct((rows, width), jnp.bfloat16),
-        grid_spec=pltpu.PrefetchScalarGridSpec(
-            num_scalar_prefetch=2,
-            grid=(rows // BLK,),
-            in_specs=[block, block, block, pl.BlockSpec(memory_space=pl.ANY), pl.BlockSpec(memory_space=pl.ANY)],
-            out_specs=block,
-            scratch_shapes=[
-                pltpu.VMEM((far_count * BLK, width), jnp.bfloat16),
-                pltpu.VMEM((far_count * BLK, width), jnp.bfloat16),
-                pltpu.VMEM((n_ctx, piece, width), jnp.bfloat16),
-                pltpu.VMEM((n_ctx, piece, width), jnp.bfloat16),
-                pltpu.SemaphoreType.DMA((far_count,)),
-                pltpu.SemaphoreType.DMA((far_count,)),
-                pltpu.SemaphoreType.DMA((2,)),
-            ],
-        ),
-        compiler_params=pltpu.CompilerParams(dimension_semantics=("arbitrary",)),
+        in_specs=[smem, smem, vmem, vmem, vmem, pl.BlockSpec(memory_space=pl.ANY), pl.BlockSpec(memory_space=pl.ANY)],
+        out_specs=vmem,
+        scratch_shapes=[
+            pltpu.VMEM((n_blocks, far_count * BLK, width), jnp.bfloat16),
+            pltpu.VMEM((n_blocks, far_count * BLK, width), jnp.bfloat16),
+            pltpu.VMEM((n_blocks, n_ctx, piece, width), jnp.bfloat16),
+            pltpu.VMEM((n_blocks, n_ctx, piece, width), jnp.bfloat16),
+            pltpu.SemaphoreType.DMA((n_blocks, far_count)),
+            pltpu.SemaphoreType.DMA((n_blocks, far_count)),
+            pltpu.SemaphoreType.DMA((n_blocks, 2)),
+        ],
     )(labels, sources, q_norm, k_norm, values, got, whole)
 
 

time: 412 us -> 410 us (level)
  transfers between devices with their start and end apart: 4 -> 4, of which waited for: 3 -> 3; matrix products, arithmetic and copies ran while one was open for 2% -> 2% of each run, Pallas kernels for 17% -> 18%
where the time goes in v9:
time: 410 us; the launch traced here: 409 us
  waiting for transfers between devices  249 us (61%)
  Pallas kernels  85.3 us (21%)
  starting transfers between devices  34 us (8%)
  between operations  14.2 us (3%)
  local copies, waits for them, and re-layouts  14 us (3%)
  other arithmetic  6.86 us (2%)
  matrix products  5.19 us (1%)
    all_to_all x1, waiting for transfers between devices, shards(): got = lax.all_to_all(send, 'ctx', 0, 0, tiled=True)  154 us
    pallas_call x1, Pallas kernels, gather_all(): pl.pallas_call(functools.partial(gather_kernel, axis, other_axis, n), out...  72 us
    unnamed x2, waiting for transfers between devices  62.3 us
    all_to_all x1, waiting for transfers between devices, shards(): lax.all_to_all(jnp.transpose(bank, (1, 0, 2, 3)), 'ctx', 0, 0, tiled=True)  32.8 us
    all_to_all x1, starting transfers between devices, shards(): got = lax.all_to_all(send, 'ctx', 0, 0, tiled=True)  17.6 us
    pallas_call x1, Pallas kernels, attend(): pl.pallas_call(attend_kernel, out_shape=jax.ShapeDtypeStruct((rows, width...  13.4 us
    all_to_all x1, starting transfers between devices, shards(): lax.all_to_all(jnp.transpose(bank, (1, 0, 2, 3)), 'ctx', 0, 0, tiled=True)  9.1 us
  transfers between devices with their start and end apart: 4, of which 3 were waited for; matrix products, arithmetic and copies ran while one was open for 2% of the time, Pallas kernels for 18%

profile of v9, /device:TPU:2, one launch (start us, length us, event | category | flops | bytes accessed | tf_op | source)
XLA Modules:
  0.0 408.8 jit_solution(17317653854795123930)
XLA Ops:
  7.2 3.5 maximum_bitcast_fusion
  10.7 9.1 %all-to-all-start.1 = ((bf16[32,2,32,640]{3,2,1,0:T(8,128)(2,1)}), bf16[32,2,32,640]{3,2,1,0:T(8,128)(2,1)S(1)}, u32[]{:S(2)}, u32[]{:S(2)}) async-start(bf16[32,2,32,640]{3,2,1,0:T(8,128)(2,1)} %maximum_bitcast_fusion), calls=%async_computation.1 | async-start | bytes 5242880 | tf_op jit(solution)/shard_map/all_to_all | solution.py:292
  19.8 32.8 %all-to-all-done.1 = bf16[32,2,32,640]{3,2,1,0:T(8,128)(2,1)S(1)} async-done(((bf16[32,2,32,640]{3,2,1,0:T(8,128)(2,1)}), bf16[32,2,32,640]{3,2,1,0:T(8,128)(2,1)S(1)}, u32[]{:S(2)}, u32[]{:S(2)}) %all-to-all-start.1) | async-done | bytes 2621472 | tf_op jit(solution)/shard_map/all_to_all | solution.py:292
  52.6 0.6 gather_fusion.1
  53.2 3.0 broadcast_in_dim.7
  56.2 0.0 copy-start.3
  56.2 7.1 %all-to-all-start.2 = ((bf16[32,128,640]{2,1,0:T(8,128)(2,1)}), bf16[32,128,640]{2,1,0:T(8,128)(2,1)}, u32[]{:S(2)}, u32[]{:S(2)}) async-start(bf16[32,128,640]{2,1,0:T(8,128)(2,1)} %broadcast_in_dim.7), calls=%async_computation.2 | async-start | bytes 10485760 | tf_op jit(solution)/shard_map/all_to_all | solution.py:297
  63.3 0.0 copy-done.2
  63.3 0.1 fusion
  63.5 0.1 fusion.3
  63.6 0.6 pad_maximum_fusion.1.piece_ref
  64.2 72.0 %shard_map.122 = f32[8,2,256]{2,1,0:T(2,128)} custom-call(f32[2,256]{1,0:T(2,128)} %pad_maximum_fusion.1.piece_ref), custom_call_target="tpu_custom_call" | custom-call | tf_op jit(solution)/shard_map/pallas_call | solution.py:130
  136.2 0.7 reduce_sum.40
  136.9 0.1 fusion.6
  137.1 0.1 fusion.5.k_ref
  137.2 0.1 pad_maximum_fusion
  137.3 5.7 %gather_fusion = bf16[32,2,128,640]{3,2,1,0:T(8,128)(2,1)} fusion(bf16[2,2,128,640]{3,2,0,1:T(8,128)(2,1)S(1)} %pad_maximum_fusion, s32[1024]{0:T(1024)S(1)} %pad_clamp_fusion.1), kind=kCustom, calls=%fused_computation | custom fusion | bytes 20971648 | tf_op jit(solution)/shard_map/gather | solution.py:289
  143.0 0.0 all-to-all-done.2.whole_ref
  143.0 17.6 %all-to-all-start = ((bf16[32,2,128,640]{3,2,1,0:T(8,128)(2,1)}), bf16[32,2,128,640]{3,2,1,0:T(8,128)(2,1)}, u32[]{:S(2)}, u32[]{:S(2)}) async-start(bf16[32,2,128,640]{3,2,1,0:T(8,128)(2,1)} %gather_fusion), calls=%async_computation | async-start | bytes 20971520 | tf_op jit(solution)/shard_map/all_to_all | solution.py:290
  160.6 0.2 reduce-scatter.4.cloned.1.call-start
  160.8 0.1 constant_dynamic-slice_fusion
  160.9 0.1 copy.14
  161.0 0.1 squeeze.3
  161.1 0.6 and_select_fusion.2.source_ref
  161.6 0.9 fusion.2.q_ref
  162.5 154.0 %all-to-all-done.got_ref = bf16[32,2,128,640]{3,2,1,0:T(8,128)(2,1)} async-done(((bf16[32,2,128,640]{3,2,1,0:T(8,128)(2,1)}), bf16[32,2,128,640]{3,2,1,0:T(8,128)(2,1)}, u32[]{:S(2)}, u32[]{:S(2)}) %all-to-all-start) | async-done | bytes 10485792 | tf_op jit(solution)/shard_map/all_to_all | solution.py:290
  316.6 13.4 %shard_map.123 = bf16[256,640]{1,0:T(8,128)(2,1)} custom-call(s32[2]{0:T(128)} %label_ref.1, s32[24]{0:T(128)} %and_select_fusion.2.source_ref, bf16[256,640]{1,0:T(8,128)(2,1)} %fusion.2.q_ref, bf16[256,640]{1,0:T(8,128)(2,1)} %copy-done, bf16[256,640]{1,0:T(8,128)(2,1)} %v_ref.1, bf16[32,2,128,640]{3,2,1,0:T(8,128)(2,1)} %all-to-all-done.got_ref, ...), custom_call_target="tpu_custom_call" | custom-call | tf_op jit(solution)/shard_map/pallas_call | solution.py:213
  329.9 5.2 %convolution_convert_fusion = bf16[256,5120]{1,0:T(8,128)(2,1)S(1)} fusion(bf16[256,640]{1,0:T(8,128)(2,1)} %shard_map.123, bf16[640,5120]{1,0:T(8,128)(2,1)} %param.18), kind=kOutput, calls=%fused_computation.2 | convolution fusion | flops 1679032320 | bytes 9502720 | tf_op jit(solution)/shard_map/dot_general | solution.py:301
  335.1 2.6 copy.15
  337.7 0.0 reduce-scatter.4.cloned.1.call-update
  337.7 62.3 %reduce-scatter.4.cloned.1.call-done = bf16[640,256]{1,0:T(8,128)(2,1)} async-done(((bf16[5120,256]{1,0:T(8,128)(2,1)}), bf16[640,256]{1,0:T(8,128)(2,1)}) %reduce-scatter.4.cloned.1.call-update) | async-done | bytes 327696
  400.0 1.9 copy.16
  (19 shorter events, 0.1 us)
Async XLA Ops:
  10.7 9.1 %copy-start.7 = (s32[2]{0:T(128)S(1)}, s32[2]{0:T(128)}, u32[]{:S(2)}) copy-start(s32[2]{0:T(128)} %param.20) | copy-start | bytes 28
  10.7 42.0 %all-to-all-start.1 = ((bf16[32,2,32,640]{3,2,1,0:T(8,128)(2,1)}), bf16[32,2,32,640]{3,2,1,0:T(8,128)(2,1)S(1)}, u32[]{:S(2)}, u32[]{:S(2)}) async-start(bf16[32,2,32,640]{3,2,1,0:T(8,128)(2,1)} %maximum_bitcast_fusion), calls=%async_computation.1 | async-start | bytes 5242880 | tf_op jit(solution)/shard_map/all_to_all | solution.py:292
  56.2 7.1 %copy-start.2 = (bf16[256,640]{1,0:T(8,128)(2,1)S(1)}, bf16[256,640]{1,0:T(8,128)(2,1)}, u32[]{:S(2)}) copy-start(bf16[256,640]{1,0:T(8,128)(2,1)} %param.11) | copy-start | bytes 983044
  56.2 7.2 %copy-start.1 = (bf16[256,640]{1,0:T(8,128)(2,1)S(1)}, bf16[256,640]{1,0:T(8,128)(2,1)}, u32[]{:S(2)}) copy-start(bf16[256,640]{1,0:T(8,128)(2,1)} %param.12) | copy-start | bytes 983044
  56.2 80.7 %copy-start.4 = (s32[32,2,12]{0,1,2:T(2,128)S(1)}, s32[32,2,12]{0,1,2:T(2,128)}, u32[]{:S(2)}) copy-start(s32[32,2,12]{0,1,2:T(2,128)} %param.19) | copy-start | bytes 9220
  56.2 80.8 %copy-start.5 = (f32[640]{0:T(1024)S(1)}, f32[640]{0:T(1024)}, u32[]{:S(2)}) copy-start(f32[640]{0:T(1024)} %param.15) | copy-start | bytes 7684
  56.2 81.0 %copy-start.3 = (bf16[256,640]{1,0:T(8,128)(2,1)S(1)}, bf16[256,640]{1,0:T(8,128)(2,1)}, u32[]{:S(2)}) copy-start(bf16[256,640]{1,0:T(8,128)(2,1)} %v_ref.1) | copy-start | bytes 983044
  56.2 86.7 %all-to-all-start.2 = ((bf16[32,128,640]{2,1,0:T(8,128)(2,1)}), bf16[32,128,640]{2,1,0:T(8,128)(2,1)}, u32[]{:S(2)}, u32[]{:S(2)}) async-start(bf16[32,128,640]{2,1,0:T(8,128)(2,1)} %broadcast_in_dim.7), calls=%async_computation.2 | async-start | bytes 10485760 | tf_op jit(solution)/shard_map/all_to_all | solution.py:297
  137.2 5.8 %copy-start = (bf16[256,640]{1,0:T(8,128)(2,1)}, bf16[256,640]{1,0:T(8,128)(2,1)S(1)}, u32[]{:S(2)}) copy-start(bf16[256,640]{1,0:T(8,128)(2,1)S(1)} %fusion.5.k_ref) | copy-start | bytes 983044
  143.0 18.7 %copy-start.6 = (f32[640]{0:T(1024)S(1)}, f32[640]{0:T(1024)}, u32[]{:S(2)}) copy-start(f32[640]{0:T(1024)} %param.14) | copy-start | bytes 7684
  143.0 173.6 %all-to-all-start = ((bf16[32,2,128,640]{3,2,1,0:T(8,128)(2,1)}), bf16[32,2,128,640]{3,2,1,0:T(8,128)(2,1)}, u32[]{:S(2)}, u32[]{:S(2)}) async-start(bf16[32,2,128,640]{3,2,1,0:T(8,128)(2,1)} %gather_fusion), calls=%async_computation | async-start | bytes 20971520 | tf_op jit(solution)/shard_map/all_to_all | solution.py:290
  160.6 239.4 %reduce-scatter.4.cloned.1.call-start = ((), (), s32[]{:S(2)}) async-start(), calls=%async_computation.4 | async-start | bytes 2949120
Sparse Core Ops, SparseCore 0:
  337.8 62.1 reduce-scatter.3

commit v10 on v9

--- a/solution.py
+++ b/solution.py
@@ -142,9 +142,11 @@
 
 
 def attend_kernel(
-    label_ref, source_ref, q_ref, k_ref, v_ref, got_ref, whole_ref, o_ref,
-    far_k, far_v, bank_k, bank_v, sem_k, sem_v, sem_bank,
+    label_ref, source_ref, q_ref, k_ref, v_ref, got_ref, whole_ref, w_hbm, o_ref, p_ref,
+    far_k, far_v, bank_k, bank_v, w_vmem, sem_k, sem_v, sem_bank, sem_w,
 ):
+    weight_copy = pltpu.make_async_copy(w_hbm, w_vmem, sem_w)
+    weight_copy.start()
     n_blocks = far_k.shape[0]
     far_count = far_k.shape[1] // BLK
     piece = bank_k.shape[2]
@@ -202,9 +204,17 @@
                 total = part_sum if total is None else total + part_sum
                 summed = product if summed is None else summed + product
             o_ref[rows, cols] = (summed / total).astype(o_ref.dtype)
-
-
-def attend(labels, sources, q_norm, k_norm, values, got, whole, n_ctx, far_count):
+    weight_copy.wait()
+    mixed_in = o_ref[...]
+    chunk = 512
+    for j in range(p_ref.shape[1] // chunk):
+        out_cols = pl.ds(j * chunk, chunk)
+        p_ref[:, out_cols] = jnp.dot(
+            mixed_in, w_vmem[:, out_cols], preferred_element_type=jnp.float32
+        ).astype(p_ref.dtype)
+
+
+def attend(labels, sources, q_norm, k_norm, values, got, whole, out_weight, n_ctx, far_count):
     rows, width = q_norm.shape
     n_blocks = rows // BLK
     piece = whole.shape[1] // 4
@@ -212,19 +222,24 @@
     smem = pl.BlockSpec(memory_space=pltpu.SMEM)
     return pl.pallas_call(
         attend_kernel,
-        out_shape=jax.ShapeDtypeStruct((rows, width), jnp.bfloat16),
-        in_specs=[smem, smem, vmem, vmem, vmem, pl.BlockSpec(memory_space=pl.ANY), pl.BlockSpec(memory_space=pl.ANY)],
-        out_specs=vmem,
+        out_shape=(
+            jax.ShapeDtypeStruct((rows, width), jnp.bfloat16),
+            jax.ShapeDtypeStruct((rows, out_weight.shape[1]), jnp.bfloat16),
+        ),
+        in_specs=[smem, smem, vmem, vmem, vmem] + [pl.BlockSpec(memory_space=pl.ANY)] * 3,
+        out_specs=(vmem, vmem),
         scratch_shapes=[
             pltpu.VMEM((n_blocks, far_count * BLK, width), jnp.bfloat16),
             pltpu.VMEM((n_blocks, far_count * BLK, width), jnp.bfloat16),
             pltpu.VMEM((n_blocks, n_ctx, piece, width), jnp.bfloat16),
             pltpu.VMEM((n_blocks, n_ctx, piece, width), jnp.bfloat16),
+            pltpu.VMEM(out_weight.shape, out_weight.dtype),
             pltpu.SemaphoreType.DMA((n_blocks, far_count)),
             pltpu.SemaphoreType.DMA((n_blocks, far_count)),
             pltpu.SemaphoreType.DMA((n_blocks, 2)),
+            pltpu.SemaphoreType.DMA(()),
         ],
-    )(labels, sources, q_norm, k_norm, values, got, whole)
+    )(labels, sources, q_norm, k_norm, values, got, whole, out_weight)
 
 
 def normalize(features, scale_gain, square_total):
@@ -297,11 +312,10 @@
     whole = lax.all_to_all(
         jnp.broadcast_to(piece_rows, (n_ctx,) + piece_rows.shape), "ctx", 0, 0, tiled=True
     )
-    attended = attend(labels, sources, q_norm, k_norm, values, got, whole, n_ctx, partners.shape[2])
-    partial_out = jnp.dot(attended, out_weight, preferred_element_type=jnp.float32)
-    mixed = lax.psum_scatter(
-        partial_out.astype(jnp.bfloat16), "head", scatter_dimension=1, tiled=True
+    attended, partial_out = attend(
+        labels, sources, q_norm, k_norm, values, got, whole, out_weight, n_ctx, partners.shape[2]
     )
+    mixed = lax.psum_scatter(partial_out, "head", scatter_dimension=1, tiled=True)
     return (attended, mixed)
 
 

time: 410 us -> 409 us (level)
  matrix products: 5.19 us -> 0 us
    dot_general x1 -> x0, matrix products: 5.19 us -> none  [shards(): jnp.dot(attended, out_weight, preferred_element_type=jnp.float32)]
where the time goes in v10:
time: 409 us; the launch traced here: 408 us
  waiting for transfers between devices  249 us (61%)
  Pallas kernels  88.4 us (22%)
  starting transfers between devices  33.8 us (8%)
  local copies, waits for them, and re-layouts  15.9 us (4%)
  between operations  14.2 us (3%)
  other arithmetic  6.81 us (2%)
    all_to_all x1, waiting for transfers between devices, shards(): got = lax.all_to_all(send, 'ctx', 0, 0, tiled=True)  154 us
    pallas_call x1, Pallas kernels, gather_all(): pl.pallas_call(functools.partial(gather_kernel, axis, other_axis, n), out...  72 us
    unnamed x2, waiting for transfers between devices  62.4 us
    all_to_all x1, waiting for transfers between devices, shards(): lax.all_to_all(jnp.transpose(bank, (1, 0, 2, 3)), 'ctx', 0, 0, tiled=True)  32.8 us
    all_to_all x1, starting transfers between devices, shards(): got = lax.all_to_all(send, 'ctx', 0, 0, tiled=True)  17.4 us
    pallas_call x1, Pallas kernels, attend(): pl.pallas_call(attend_kernel, out_shape=(jax.ShapeDtypeStruct((rows, widt...  16.4 us
    all_to_all x1, starting transfers between devices, shards(): lax.all_to_all(jnp.transpose(bank, (1, 0, 2, 3)), 'ctx', 0, 0, tiled=True)  9.1 us
  transfers between devices with their start and end apart: 4, of which 3 were waited for; matrix products, arithmetic and copies ran while one was open for 2% of the time, Pallas kernels for 18%

profile of v10, /device:TPU:2, one launch (start us, length us, event | category | flops | bytes accessed | tf_op | source)
XLA Modules:
  0.0 408.4 jit_solution(6331681583025696172)
XLA Ops:
  7.2 3.5 maximum_bitcast_fusion
  10.7 9.1 %all-to-all-start.1 = ((bf16[32,2,32,640]{3,2,1,0:T(8,128)(2,1)}), bf16[32,2,32,640]{3,2,1,0:T(8,128)(2,1)S(1)}, u32[]{:S(2)}, u32[]{:S(2)}) async-start(bf16[32,2,32,640]{3,2,1,0:T(8,128)(2,1)} %maximum_bitcast_fusion), calls=%async_computation.1 | async-start | bytes 5242880 | tf_op jit(solution)/shard_map/all_to_all | solution.py:307
  19.8 32.8 %all-to-all-done.1 = bf16[32,2,32,640]{3,2,1,0:T(8,128)(2,1)S(1)} async-done(((bf16[32,2,32,640]{3,2,1,0:T(8,128)(2,1)}), bf16[32,2,32,640]{3,2,1,0:T(8,128)(2,1)S(1)}, u32[]{:S(2)}, u32[]{:S(2)}) %all-to-all-start.1) | async-done | bytes 2621472 | tf_op jit(solution)/shard_map/all_to_all | solution.py:307
  52.6 0.6 gather_fusion.1
  53.2 3.0 broadcast_in_dim.7
  56.2 0.0 copy-start.3
  56.2 7.1 %all-to-all-start.2 = ((bf16[32,128,640]{2,1,0:T(8,128)(2,1)}), bf16[32,128,640]{2,1,0:T(8,128)(2,1)}, u32[]{:S(2)}, u32[]{:S(2)}) async-start(bf16[32,128,640]{2,1,0:T(8,128)(2,1)} %broadcast_in_dim.7), calls=%async_computation.2 | async-start | bytes 10485760 | tf_op jit(solution)/shard_map/all_to_all | solution.py:312
  63.3 0.0 copy-done.2
  63.3 0.1 fusion
  63.5 0.0 copy-done.1
  63.5 0.1 fusion.3
  63.6 0.6 pad_maximum_fusion.1.piece_ref
  64.2 72.0 %shard_map.122 = f32[8,2,256]{2,1,0:T(2,128)} custom-call(f32[2,256]{1,0:T(2,128)} %pad_maximum_fusion.1.piece_ref), custom_call_target="tpu_custom_call" | custom-call | tf_op jit(solution)/shard_map/pallas_call | solution.py:130
  136.2 0.7 reduce_sum.40
  136.9 0.1 fusion.6
  137.1 0.1 fusion.5.k_ref
  137.2 0.1 pad_maximum_fusion
  137.3 5.8 %gather_fusion = bf16[32,2,128,640]{3,2,1,0:T(8,128)(2,1)} fusion(bf16[2,2,128,640]{3,2,0,1:T(8,128)(2,1)S(1)} %pad_maximum_fusion, s32[1024]{0:T(1024)S(1)} %pad_clamp_fusion.1), kind=kCustom, calls=%fused_computation | custom fusion | bytes 20971648 | tf_op jit(solution)/shard_map/gather | solution.py:304
  143.1 0.0 all-to-all-done.2.whole_ref
  143.1 17.4 %all-to-all-start = ((bf16[32,2,128,640]{3,2,1,0:T(8,128)(2,1)}), bf16[32,2,128,640]{3,2,1,0:T(8,128)(2,1)}, u32[]{:S(2)}, u32[]{:S(2)}) async-start(bf16[32,2,128,640]{3,2,1,0:T(8,128)(2,1)} %gather_fusion), calls=%async_computation | async-start | bytes 20971520 | tf_op jit(solution)/shard_map/all_to_all | solution.py:305
  160.6 0.2 reduce-scatter.4.cloned.1.call-start
  160.8 0.1 constant_dynamic-slice_fusion
  160.9 0.1 copy.14
  161.0 0.1 squeeze.3
  161.1 0.5 and_select_fusion.2.source_ref
  161.6 0.9 fusion.2.q_ref
  162.4 154.1 %all-to-all-done.got_ref = bf16[32,2,128,640]{3,2,1,0:T(8,128)(2,1)} async-done(((bf16[32,2,128,640]{3,2,1,0:T(8,128)(2,1)}), bf16[32,2,128,640]{3,2,1,0:T(8,128)(2,1)}, u32[]{:S(2)}, u32[]{:S(2)}) %all-to-all-start) | async-done | bytes 10485792 | tf_op jit(solution)/shard_map/all_to_all | solution.py:305
  316.5 16.4 %shard_map.123 = (bf16[256,640]{1,0:T(8,128)(2,1)}, bf16[256,5120]{1,0:T(8,128)(2,1)}) custom-call(s32[2]{0:T(128)} %label_ref.1, s32[24]{0:T(128)} %and_select_fusion.2.source_ref, bf16[256,640]{1,0:T(8,128)(2,1)} %fusion.2.q_ref, bf16[256,640]{1,0:T(8,128)(2,1)} %copy-done, bf16[256,640]{1,0:T(8,128)(2,1)} %v_ref.1, ...), custom_call_target="tpu_custom_call" | custom-call | tf_op jit(solution)/shard_map/pallas_call | solution.py:223
  332.9 4.4 %copy.15 = bf16[256,5120]{0,1:T(8,128)(2,1)} copy(bf16[256,5120]{1,0:T(8,128)(2,1)} %get-tuple-element.5) | data formatting | bytes 5242880
  337.3 0.0 reduce-scatter.4.cloned.1.call-update
  337.3 62.3 %reduce-scatter.4.cloned.1.call-done = bf16[640,256]{1,0:T(8,128)(2,1)} async-done(((bf16[5120,256]{1,0:T(8,128)(2,1)}), bf16[640,256]{1,0:T(8,128)(2,1)}) %reduce-scatter.4.cloned.1.call-update) | async-done | bytes 327696
  399.7 1.9 copy.16
  (18 shorter events, 0.1 us)
Async XLA Ops:
  10.7 9.1 %copy-start.7 = (s32[2]{0:T(128)S(1)}, s32[2]{0:T(128)}, u32[]{:S(2)}) copy-start(s32[2]{0:T(128)} %param.20) | copy-start | bytes 28
  10.7 42.0 %all-to-all-start.1 = ((bf16[32,2,32,640]{3,2,1,0:T(8,128)(2,1)}), bf16[32,2,32,640]{3,2,1,0:T(8,128)(2,1)S(1)}, u32[]{:S(2)}, u32[]{:S(2)}) async-start(bf16[32,2,32,640]{3,2,1,0:T(8,128)(2,1)} %maximum_bitcast_fusion), calls=%async_computation.1 | async-start | bytes 5242880 | tf_op jit(solution)/shard_map/all_to_all | solution.py:307
  56.2 7.1 %copy-start.2 = (bf16[256,640]{1,0:T(8,128)(2,1)S(1)}, bf16[256,640]{1,0:T(8,128)(2,1)}, u32[]{:S(2)}) copy-start(bf16[256,640]{1,0:T(8,128)(2,1)} %param.11) | copy-start | bytes 983044
  56.2 7.2 %copy-start.1 = (bf16[256,640]{1,0:T(8,128)(2,1)S(1)}, bf16[256,640]{1,0:T(8,128)(2,1)}, u32[]{:S(2)}) copy-start(bf16[256,640]{1,0:T(8,128)(2,1)} %param.12) | copy-start | bytes 983044
  56.2 80.7 %copy-start.4 = (s32[32,2,12]{0,1,2:T(2,128)S(1)}, s32[32,2,12]{0,1,2:T(2,128)}, u32[]{:S(2)}) copy-start(s32[32,2,12]{0,1,2:T(2,128)} %param.19) | copy-start | bytes 9220
  56.2 80.8 %copy-start.5 = (f32[640]{0:T(1024)S(1)}, f32[640]{0:T(1024)}, u32[]{:S(2)}) copy-start(f32[640]{0:T(1024)} %param.15) | copy-start | bytes 7684
  56.2 81.0 %copy-start.3 = (bf16[256,640]{1,0:T(8,128)(2,1)S(1)}, bf16[256,640]{1,0:T(8,128)(2,1)}, u32[]{:S(2)}) copy-start(bf16[256,640]{1,0:T(8,128)(2,1)} %v_ref.1) | copy-start | bytes 983044
  56.2 86.9 %all-to-all-start.2 = ((bf16[32,128,640]{2,1,0:T(8,128)(2,1)}), bf16[32,128,640]{2,1,0:T(8,128)(2,1)}, u32[]{:S(2)}, u32[]{:S(2)}) async-start(bf16[32,128,640]{2,1,0:T(8,128)(2,1)} %broadcast_in_dim.7), calls=%async_computation.2 | async-start | bytes 10485760 | tf_op jit(solution)/shard_map/all_to_all | solution.py:312
  137.2 5.9 %copy-start = (bf16[256,640]{1,0:T(8,128)(2,1)}, bf16[256,640]{1,0:T(8,128)(2,1)S(1)}, u32[]{:S(2)}) copy-start(bf16[256,640]{1,0:T(8,128)(2,1)S(1)} %fusion.5.k_ref) | copy-start | bytes 983044
  143.1 18.5 %copy-start.6 = (f32[640]{0:T(1024)S(1)}, f32[640]{0:T(1024)}, u32[]{:S(2)}) copy-start(f32[640]{0:T(1024)} %param.14) | copy-start | bytes 7684
  143.1 173.4 %all-to-all-start = ((bf16[32,2,128,640]{3,2,1,0:T(8,128)(2,1)}), bf16[32,2,128,640]{3,2,1,0:T(8,128)(2,1)}, u32[]{:S(2)}, u32[]{:S(2)}) async-start(bf16[32,2,128,640]{3,2,1,0:T(8,128)(2,1)} %gather_fusion), calls=%async_computation | async-start | bytes 20971520 | tf_op jit(solution)/shard_map/all_to_all | solution.py:305
  160.6 239.1 %reduce-scatter.4.cloned.1.call-start = ((), (), s32[]{:S(2)}) async-start(), calls=%async_computation.4 | async-start | bytes 2949120
Sparse Core Ops, SparseCore 0:
  337.5 62.1 reduce-scatter.3

commit v11 on v10

--- a/solution.py
+++ b/solution.py
@@ -207,11 +207,11 @@
     weight_copy.wait()
     mixed_in = o_ref[...]
     chunk = 512
-    for j in range(p_ref.shape[1] // chunk):
+    for j in range(p_ref.shape[0] // chunk):
         out_cols = pl.ds(j * chunk, chunk)
-        p_ref[:, out_cols] = jnp.dot(
+        p_ref[out_cols, :] = jnp.dot(
             mixed_in, w_vmem[:, out_cols], preferred_element_type=jnp.float32
-        ).astype(p_ref.dtype)
+        ).T.astype(p_ref.dtype)
 
 
 def attend(labels, sources, q_norm, k_norm, values, got, whole, out_weight, n_ctx, far_count):
@@ -224,7 +224,7 @@
         attend_kernel,
         out_shape=(
             jax.ShapeDtypeStruct((rows, width), jnp.bfloat16),
-            jax.ShapeDtypeStruct((rows, out_weight.shape[1]), jnp.bfloat16),
+            jax.ShapeDtypeStruct((out_weight.shape[1], rows), jnp.bfloat16),
         ),
         in_specs=[smem, smem, vmem, vmem, vmem] + [pl.BlockSpec(memory_space=pl.ANY)] * 3,
         out_specs=(vmem, vmem),
@@ -315,7 +315,7 @@
     attended, partial_out = attend(
         labels, sources, q_norm, k_norm, values, got, whole, out_weight, n_ctx, partners.shape[2]
     )
-    mixed = lax.psum_scatter(partial_out, "head", scatter_dimension=1, tiled=True)
+    mixed = lax.psum_scatter(partial_out, "head", scatter_dimension=0, tiled=True).T
     return (attended, mixed)
 
 

time: 409 us -> 405 us (level)
  local copies, waits for them, and re-layouts: 15.9 us -> 11.5 us
    reduce_scatter x0 -> x1, waiting for transfers between devices: none -> 62.4 us  [shards(): lax.psum_scatter(partial_out, 'head', scatter_dimension=0, tiled=True)]
    unnamed x2 -> x1, waiting for transfers between devices: 62.4 us -> 0.02 us
    unnamed x18 -> x17, local copies, waits for them, and re-layouts: 6.29 us -> 1.9 us
where the time goes in v11:
time: 405 us; the launch traced here: 404 us
  waiting for transfers between devices  249 us (61%)
  Pallas kernels  88.4 us (22%)
  starting transfers between devices  33.9 us (8%)
  between operations  14.2 us (4%)
  local copies, waits for them, and re-layouts  11.5 us (3%)
  other arithmetic  6.81 us (2%)
    all_to_all x1, waiting for transfers between devices, shards(): got = lax.all_to_all(send, 'ctx', 0, 0, tiled=True)  154 us
    pallas_call x1, Pallas kernels, gather_all(): pl.pallas_call(functools.partial(gather_kernel, axis, other_axis, n), out...  72 us
    reduce_scatter x1, waiting for transfers between devices, shards(): lax.psum_scatter(partial_out, 'head', scatter_dimension=0, tiled=True)  62.4 us
    all_to_all x1, waiting for transfers between devices, shards(): lax.all_to_all(jnp.transpose(bank, (1, 0, 2, 3)), 'ctx', 0, 0, tiled=True)  32.8 us
    all_to_all x1, starting transfers between devices, shards(): got = lax.all_to_all(send, 'ctx', 0, 0, tiled=True)  17.5 us
    pallas_call x1, Pallas kernels, attend(): pl.pallas_call(attend_kernel, out_shape=(jax.ShapeDtypeStruct((rows, widt...  16.5 us
    all_to_all x1, starting transfers between devices, shards(): lax.all_to_all(jnp.transpose(bank, (1, 0, 2, 3)), 'ctx', 0, 0, tiled=True)  9.1 us
  transfers between devices with their start and end apart: 4, of which 3 were waited for; matrix products, arithmetic and copies ran while one was open for 2% of the time, Pallas kernels for 18%

profile of v11, /device:TPU:2, one launch (start us, length us, event | category | flops | bytes accessed | tf_op | source)
XLA Modules:
  0.0 404.2 jit_solution(16106410696245365159)
XLA Ops:
  7.2 3.5 maximum_bitcast_fusion
  10.7 9.1 %all-to-all-start.1 = ((bf16[32,2,32,640]{3,2,1,0:T(8,128)(2,1)}), bf16[32,2,32,640]{3,2,1,0:T(8,128)(2,1)S(1)}, u32[]{:S(2)}, u32[]{:S(2)}) async-start(bf16[32,2,32,640]{3,2,1,0:T(8,128)(2,1)} %maximum_bitcast_fusion), calls=%async_computation.1 | async-start | bytes 5242880 | tf_op jit(solution)/shard_map/all_to_all | solution.py:307
  19.8 32.8 %all-to-all-done.1 = bf16[32,2,32,640]{3,2,1,0:T(8,128)(2,1)S(1)} async-done(((bf16[32,2,32,640]{3,2,1,0:T(8,128)(2,1)}), bf16[32,2,32,640]{3,2,1,0:T(8,128)(2,1)S(1)}, u32[]{:S(2)}, u32[]{:S(2)}) %all-to-all-start.1) | async-done | bytes 2621472 | tf_op jit(solution)/shard_map/all_to_all | solution.py:307
  52.6 0.6 gather_fusion.1
  53.2 3.0 broadcast_in_dim.7
  56.2 0.0 copy-start.3
  56.2 7.1 %all-to-all-start.2 = ((bf16[32,128,640]{2,1,0:T(8,128)(2,1)}), bf16[32,128,640]{2,1,0:T(8,128)(2,1)}, u32[]{:S(2)}, u32[]{:S(2)}) async-start(bf16[32,128,640]{2,1,0:T(8,128)(2,1)} %broadcast_in_dim.7), calls=%async_computation.2 | async-start | bytes 10485760 | tf_op jit(solution)/shard_map/all_to_all | solution.py:312
  63.3 0.0 copy-done.2
  63.3 0.1 fusion
  63.5 0.1 fusion.3
  63.6 0.6 pad_maximum_fusion.1.piece_ref
  64.2 72.0 %shard_map.122 = f32[8,2,256]{2,1,0:T(2,128)} custom-call(f32[2,256]{1,0:T(2,128)} %pad_maximum_fusion.1.piece_ref), custom_call_target="tpu_custom_call" | custom-call | tf_op jit(solution)/shard_map/pallas_call | solution.py:130
  136.2 0.7 reduce_sum.40
  136.9 0.1 fusion.6
  137.0 0.0 copy-done.5
  137.1 0.1 fusion.5.k_ref
  137.2 0.1 pad_maximum_fusion
  137.3 5.8 %gather_fusion = bf16[32,2,128,640]{3,2,1,0:T(8,128)(2,1)} fusion(bf16[2,2,128,640]{3,2,0,1:T(8,128)(2,1)S(1)} %pad_maximum_fusion, s32[1024]{0:T(1024)S(1)} %pad_clamp_fusion.1), kind=kCustom, calls=%fused_computation | custom fusion | bytes 20971648 | tf_op jit(solution)/shard_map/gather | solution.py:304
  143.1 0.0 copy-done
  143.1 0.0 all-to-all-done.2.whole_ref
  143.1 17.5 %all-to-all-start = ((bf16[32,2,128,640]{3,2,1,0:T(8,128)(2,1)}), bf16[32,2,128,640]{3,2,1,0:T(8,128)(2,1)}, u32[]{:S(2)}, u32[]{:S(2)}) async-start(bf16[32,2,128,640]{3,2,1,0:T(8,128)(2,1)} %gather_fusion), calls=%async_computation | async-start | bytes 20971520 | tf_op jit(solution)/shard_map/all_to_all | solution.py:305
  160.6 0.2 reduce-scatter.2.cloned.1.call-start
  160.9 0.1 constant_dynamic-slice_fusion
  161.0 0.1 copy.15
  161.1 0.1 squeeze.3
  161.1 0.5 and_select_fusion.2.source_ref
  161.7 0.9 fusion.2.q_ref
  162.5 154.1 %all-to-all-done.got_ref = bf16[32,2,128,640]{3,2,1,0:T(8,128)(2,1)} async-done(((bf16[32,2,128,640]{3,2,1,0:T(8,128)(2,1)}), bf16[32,2,128,640]{3,2,1,0:T(8,128)(2,1)}, u32[]{:S(2)}, u32[]{:S(2)}) %all-to-all-start) | async-done | bytes 10485792 | tf_op jit(solution)/shard_map/all_to_all | solution.py:305
  316.6 16.5 %shard_map.123 = (bf16[256,640]{1,0:T(8,128)(2,1)}, bf16[5120,256]{1,0:T(8,128)(2,1)}) custom-call(s32[2]{0:T(128)} %label_ref.1, s32[24]{0:T(128)} %and_select_fusion.2.source_ref, bf16[256,640]{1,0:T(8,128)(2,1)} %fusion.2.q_ref, bf16[256,640]{1,0:T(8,128)(2,1)} %copy-done, bf16[256,640]{1,0:T(8,128)(2,1)} %v_ref.1, ...), custom_call_target="tpu_custom_call" | custom-call | tf_op jit(solution)/shard_map/pallas_call | solution.py:223
  333.1 0.0 reduce-scatter.2.cloned.1.call-update
  333.1 62.4 %reduce-scatter.2.cloned.1.call-done = bf16[640,256]{1,0:T(8,128)(2,1)} async-done(((bf16[5120,256]{1,0:T(8,128)(2,1)}), bf16[640,256]{1,0:T(8,128)(2,1)}) %reduce-scatter.2.cloned.1.call-update) | async-done | bytes 327696 | tf_op jit(solution)/shard_map/reduce_scatter | solution.py:318
  395.5 1.9 copy.16
  (17 shorter events, 0.1 us)
Async XLA Ops:
  10.7 9.1 %copy-start.7 = (s32[2]{0:T(128)S(1)}, s32[2]{0:T(128)}, u32[]{:S(2)}) copy-start(s32[2]{0:T(128)} %param.20) | copy-start | bytes 28
  10.7 42.0 %all-to-all-start.1 = ((bf16[32,2,32,640]{3,2,1,0:T(8,128)(2,1)}), bf16[32,2,32,640]{3,2,1,0:T(8,128)(2,1)S(1)}, u32[]{:S(2)}, u32[]{:S(2)}) async-start(bf16[32,2,32,640]{3,2,1,0:T(8,128)(2,1)} %maximum_bitcast_fusion), calls=%async_computation.1 | async-start | bytes 5242880 | tf_op jit(solution)/shard_map/all_to_all | solution.py:307
  56.2 7.1 %copy-start.2 = (bf16[256,640]{1,0:T(8,128)(2,1)S(1)}, bf16[256,640]{1,0:T(8,128)(2,1)}, u32[]{:S(2)}) copy-start(bf16[256,640]{1,0:T(8,128)(2,1)} %param.11) | copy-start | bytes 983044
  56.2 7.2 %copy-start.1 = (bf16[256,640]{1,0:T(8,128)(2,1)S(1)}, bf16[256,640]{1,0:T(8,128)(2,1)}, u32[]{:S(2)}) copy-start(bf16[256,640]{1,0:T(8,128)(2,1)} %param.12) | copy-start | bytes 983044
  56.2 80.7 %copy-start.4 = (s32[32,2,12]{0,1,2:T(2,128)S(1)}, s32[32,2,12]{0,1,2:T(2,128)}, u32[]{:S(2)}) copy-start(s32[32,2,12]{0,1,2:T(2,128)} %param.19) | copy-start | bytes 9220
  56.2 80.8 %copy-start.5 = (f32[640]{0:T(1024)S(1)}, f32[640]{0:T(1024)}, u32[]{:S(2)}) copy-start(f32[640]{0:T(1024)} %param.15) | copy-start | bytes 7684
  56.2 81.0 %copy-start.3 = (bf16[256,640]{1,0:T(8,128)(2,1)S(1)}, bf16[256,640]{1,0:T(8,128)(2,1)}, u32[]{:S(2)}) copy-start(bf16[256,640]{1,0:T(8,128)(2,1)} %v_ref.1) | copy-start | bytes 983044
  56.2 86.9 %all-to-all-start.2 = ((bf16[32,128,640]{2,1,0:T(8,128)(2,1)}), bf16[32,128,640]{2,1,0:T(8,128)(2,1)}, u32[]{:S(2)}, u32[]{:S(2)}) async-start(bf16[32,128,640]{2,1,0:T(8,128)(2,1)} %broadcast_in_dim.7), calls=%async_computation.2 | async-start | bytes 10485760 | tf_op jit(solution)/shard_map/all_to_all | solution.py:312
  137.2 5.9 %copy-start = (bf16[256,640]{1,0:T(8,128)(2,1)}, bf16[256,640]{1,0:T(8,128)(2,1)S(1)}, u32[]{:S(2)}) copy-start(bf16[256,640]{1,0:T(8,128)(2,1)S(1)} %fusion.5.k_ref) | copy-start | bytes 983044
  143.1 18.6 %copy-start.6 = (f32[640]{0:T(1024)S(1)}, f32[640]{0:T(1024)}, u32[]{:S(2)}) copy-start(f32[640]{0:T(1024)} %param.14) | copy-start | bytes 7684
  143.1 173.5 %all-to-all-start = ((bf16[32,2,128,640]{3,2,1,0:T(8,128)(2,1)}), bf16[32,2,128,640]{3,2,1,0:T(8,128)(2,1)}, u32[]{:S(2)}, u32[]{:S(2)}) async-start(bf16[32,2,128,640]{3,2,1,0:T(8,128)(2,1)} %gather_fusion), calls=%async_computation | async-start | bytes 20971520 | tf_op jit(solution)/shard_map/all_to_all | solution.py:305
  160.6 234.9 %reduce-scatter.2.cloned.1.call-start = ((), (), s32[]{:S(2)}) async-start(), calls=%async_computation.4 | async-start | bytes 2949120 | tf_op jit(solution)/shard_map/reduce_scatter | solution.py:318
Sparse Core Ops, SparseCore 0:
  333.2 62.2 reduce-scatter.1

commit v12 on v11

--- a/solution.py
+++ b/solution.py
@@ -145,8 +145,7 @@
     label_ref, source_ref, q_ref, k_ref, v_ref, got_ref, whole_ref, w_hbm, o_ref, p_ref,
     far_k, far_v, bank_k, bank_v, w_vmem, sem_k, sem_v, sem_bank, sem_w,
 ):
-    weight_copy = pltpu.make_async_copy(w_hbm, w_vmem, sem_w)
-    weight_copy.start()
+
     n_blocks = far_k.shape[0]
     far_count = far_k.shape[1] // BLK
     piece = bank_k.shape[2]
@@ -170,6 +169,8 @@
         for copy in copies:
             copy.start()
         pending.append(copies)
+    weight_copy = pltpu.make_async_copy(w_hbm, w_vmem, sem_w)
+    weight_copy.start()
     width = q_ref.shape[1]
     bank_rows = bank_k.shape[1] * piece
     dims = (((1,), (1,)), ((), ()))

time: 405 us -> 405 us (level)
  no operation moved by 1% of the time
where the time goes in v12:
time: 405 us; the launch traced here: 404 us
  waiting for transfers between devices  249 us (61%)
  Pallas kernels  88.4 us (22%)
  starting transfers between devices  33.8 us (8%)
  between operations  14.2 us (4%)
  local copies, waits for them, and re-layouts  11.5 us (3%)
  other arithmetic  6.81 us (2%)
    all_to_all x1, waiting for transfers between devices, shards(): got = lax.all_to_all(send, 'ctx', 0, 0, tiled=True)  154 us
    pallas_call x1, Pallas kernels, gather_all(): pl.pallas_call(functools.partial(gather_kernel, axis, other_axis, n), out...  72 us
    reduce_scatter x1, waiting for transfers between devices, shards(): lax.psum_scatter(partial_out, 'head', scatter_dimension=0, tiled=True)  62.1 us
    all_to_all x1, waiting for transfers between devices, shards(): lax.all_to_all(jnp.transpose(bank, (1, 0, 2, 3)), 'ctx', 0, 0, tiled=True)  32.8 us
    all_to_all x1, starting transfers between devices, shards(): got = lax.all_to_all(send, 'ctx', 0, 0, tiled=True)  17.5 us
    pallas_call x1, Pallas kernels, attend(): pl.pallas_call(attend_kernel, out_shape=(jax.ShapeDtypeStruct((rows, widt...  16.5 us
    all_to_all x1, starting transfers between devices, shards(): lax.all_to_all(jnp.transpose(bank, (1, 0, 2, 3)), 'ctx', 0, 0, tiled=True)  9.1 us
  transfers between devices with their start and end apart: 4, of which 3 were waited for; matrix products, arithmetic and copies ran while one was open for 2% of the time, Pallas kernels for 18%

profile of v12, /device:TPU:2, one launch (start us, length us, event | category | flops | bytes accessed | tf_op | source)
XLA Modules:
  0.0 403.8 jit_solution(7384781875060309094)
XLA Ops:
  7.2 3.5 maximum_bitcast_fusion
  10.7 9.1 %all-to-all-start.1 = ((bf16[32,2,32,640]{3,2,1,0:T(8,128)(2,1)}), bf16[32,2,32,640]{3,2,1,0:T(8,128)(2,1)S(1)}, u32[]{:S(2)}, u32[]{:S(2)}) async-start(bf16[32,2,32,640]{3,2,1,0:T(8,128)(2,1)} %maximum_bitcast_fusion), calls=%async_computation.1 | async-start | bytes 5242880 | tf_op jit(solution)/shard_map/all_to_all | solution.py:308
  19.8 0.0 copy-done.7
  19.8 32.8 %all-to-all-done.1 = bf16[32,2,32,640]{3,2,1,0:T(8,128)(2,1)S(1)} async-done(((bf16[32,2,32,640]{3,2,1,0:T(8,128)(2,1)}), bf16[32,2,32,640]{3,2,1,0:T(8,128)(2,1)S(1)}, u32[]{:S(2)}, u32[]{:S(2)}) %all-to-all-start.1) | async-done | bytes 2621472 | tf_op jit(solution)/shard_map/all_to_all | solution.py:308
  52.6 0.6 gather_fusion.1
  53.2 3.0 broadcast_in_dim.7
  56.2 0.0 copy-start.3
  56.2 7.1 %all-to-all-start.2 = ((bf16[32,128,640]{2,1,0:T(8,128)(2,1)}), bf16[32,128,640]{2,1,0:T(8,128)(2,1)}, u32[]{:S(2)}, u32[]{:S(2)}) async-start(bf16[32,128,640]{2,1,0:T(8,128)(2,1)} %broadcast_in_dim.7), calls=%async_computation.2 | async-start | bytes 10485760 | tf_op jit(solution)/shard_map/all_to_all | solution.py:313
  63.3 0.1 fusion
  63.5 0.1 fusion.3
  63.6 0.6 pad_maximum_fusion.1.piece_ref
  64.2 72.0 %shard_map.122 = f32[8,2,256]{2,1,0:T(2,128)} custom-call(f32[2,256]{1,0:T(2,128)} %pad_maximum_fusion.1.piece_ref), custom_call_target="tpu_custom_call" | custom-call | tf_op jit(solution)/shard_map/pallas_call | solution.py:130
  136.2 0.7 reduce_sum.40
  136.9 0.1 fusion.6
  137.0 0.0 copy-done.5
  137.1 0.1 fusion.5.k_ref
  137.2 0.0 copy-start
  137.2 0.1 pad_maximum_fusion
  137.3 5.8 %gather_fusion = bf16[32,2,128,640]{3,2,1,0:T(8,128)(2,1)} fusion(bf16[2,2,128,640]{3,2,0,1:T(8,128)(2,1)S(1)} %pad_maximum_fusion, s32[1024]{0:T(1024)S(1)} %pad_clamp_fusion.1), kind=kCustom, calls=%fused_computation | custom fusion | bytes 20971648 | tf_op jit(solution)/shard_map/gather | solution.py:305
  143.1 0.0 all-to-all-done.2.whole_ref
  143.1 17.5 %all-to-all-start = ((bf16[32,2,128,640]{3,2,1,0:T(8,128)(2,1)}), bf16[32,2,128,640]{3,2,1,0:T(8,128)(2,1)}, u32[]{:S(2)}, u32[]{:S(2)}) async-start(bf16[32,2,128,640]{3,2,1,0:T(8,128)(2,1)} %gather_fusion), calls=%async_computation | async-start | bytes 20971520 | tf_op jit(solution)/shard_map/all_to_all | solution.py:306
  160.6 0.2 reduce-scatter.2.cloned.1.call-start
  160.8 0.1 constant_dynamic-slice_fusion
  160.9 0.1 copy.15
  161.0 0.1 squeeze.3
  161.1 0.5 and_select_fusion.2.source_ref
  161.6 0.9 fusion.2.q_ref
  162.4 154.1 %all-to-all-done.got_ref = bf16[32,2,128,640]{3,2,1,0:T(8,128)(2,1)} async-done(((bf16[32,2,128,640]{3,2,1,0:T(8,128)(2,1)}), bf16[32,2,128,640]{3,2,1,0:T(8,128)(2,1)}, u32[]{:S(2)}, u32[]{:S(2)}) %all-to-all-start) | async-done | bytes 10485792 | tf_op jit(solution)/shard_map/all_to_all | solution.py:306
  316.5 16.5 %shard_map.123 = (bf16[256,640]{1,0:T(8,128)(2,1)}, bf16[5120,256]{1,0:T(8,128)(2,1)}) custom-call(s32[2]{0:T(128)} %label_ref.1, s32[24]{0:T(128)} %and_select_fusion.2.source_ref, bf16[256,640]{1,0:T(8,128)(2,1)} %fusion.2.q_ref, bf16[256,640]{1,0:T(8,128)(2,1)} %copy-done, bf16[256,640]{1,0:T(8,128)(2,1)} %v_ref.1, ...), custom_call_target="tpu_custom_call" | custom-call | tf_op jit(solution)/shard_map/pallas_call | solution.py:224
  333.0 0.0 reduce-scatter.2.cloned.1.call-update
  333.0 62.1 %reduce-scatter.2.cloned.1.call-done = bf16[640,256]{1,0:T(8,128)(2,1)} async-done(((bf16[5120,256]{1,0:T(8,128)(2,1)}), bf16[640,256]{1,0:T(8,128)(2,1)}) %reduce-scatter.2.cloned.1.call-update) | async-done | bytes 327696 | tf_op jit(solution)/shard_map/reduce_scatter | solution.py:319
  395.1 1.9 copy.16
  (17 shorter events, 0.1 us)
Async XLA Ops:
  10.7 9.1 %copy-start.7 = (s32[2]{0:T(128)S(1)}, s32[2]{0:T(128)}, u32[]{:S(2)}) copy-start(s32[2]{0:T(128)} %param.20) | copy-start | bytes 28
  10.7 42.0 %all-to-all-start.1 = ((bf16[32,2,32,640]{3,2,1,0:T(8,128)(2,1)}), bf16[32,2,32,640]{3,2,1,0:T(8,128)(2,1)S(1)}, u32[]{:S(2)}, u32[]{:S(2)}) async-start(bf16[32,2,32,640]{3,2,1,0:T(8,128)(2,1)} %maximum_bitcast_fusion), calls=%async_computation.1 | async-start | bytes 5242880 | tf_op jit(solution)/shard_map/all_to_all | solution.py:308
  56.2 7.1 %copy-start.2 = (bf16[256,640]{1,0:T(8,128)(2,1)S(1)}, bf16[256,640]{1,0:T(8,128)(2,1)}, u32[]{:S(2)}) copy-start(bf16[256,640]{1,0:T(8,128)(2,1)} %param.11) | copy-start | bytes 983044
  56.2 7.2 %copy-start.1 = (bf16[256,640]{1,0:T(8,128)(2,1)S(1)}, bf16[256,640]{1,0:T(8,128)(2,1)}, u32[]{:S(2)}) copy-start(bf16[256,640]{1,0:T(8,128)(2,1)} %param.12) | copy-start | bytes 983044
  56.2 80.7 %copy-start.4 = (s32[32,2,12]{0,1,2:T(2,128)S(1)}, s32[32,2,12]{0,1,2:T(2,128)}, u32[]{:S(2)}) copy-start(s32[32,2,12]{0,1,2:T(2,128)} %param.19) | copy-start | bytes 9220
  56.2 80.8 %copy-start.5 = (f32[640]{0:T(1024)S(1)}, f32[640]{0:T(1024)}, u32[]{:S(2)}) copy-start(f32[640]{0:T(1024)} %param.15) | copy-start | bytes 7684
  56.2 81.0 %copy-start.3 = (bf16[256,640]{1,0:T(8,128)(2,1)S(1)}, bf16[256,640]{1,0:T(8,128)(2,1)}, u32[]{:S(2)}) copy-start(bf16[256,640]{1,0:T(8,128)(2,1)} %v_ref.1) | copy-start | bytes 983044
  56.2 86.8 %all-to-all-start.2 = ((bf16[32,128,640]{2,1,0:T(8,128)(2,1)}), bf16[32,128,640]{2,1,0:T(8,128)(2,1)}, u32[]{:S(2)}, u32[]{:S(2)}) async-start(bf16[32,128,640]{2,1,0:T(8,128)(2,1)} %broadcast_in_dim.7), calls=%async_computation.2 | async-start | bytes 10485760 | tf_op jit(solution)/shard_map/all_to_all | solution.py:313
  137.2 5.9 %copy-start = (bf16[256,640]{1,0:T(8,128)(2,1)}, bf16[256,640]{1,0:T(8,128)(2,1)S(1)}, u32[]{:S(2)}) copy-start(bf16[256,640]{1,0:T(8,128)(2,1)S(1)} %fusion.5.k_ref) | copy-start | bytes 983044
  143.1 18.5 %copy-start.6 = (f32[640]{0:T(1024)S(1)}, f32[640]{0:T(1024)}, u32[]{:S(2)}) copy-start(f32[640]{0:T(1024)} %param.14) | copy-start | bytes 7684
  143.1 173.4 %all-to-all-start = ((bf16[32,2,128,640]{3,2,1,0:T(8,128)(2,1)}), bf16[32,2,128,640]{3,2,1,0:T(8,128)(2,1)}, u32[]{:S(2)}, u32[]{:S(2)}) async-start(bf16[32,2,128,640]{3,2,1,0:T(8,128)(2,1)} %gather_fusion), calls=%async_computation | async-start | bytes 20971520 | tf_op jit(solution)/shard_map/all_to_all | solution.py:306
  160.6 234.6 %reduce-scatter.2.cloned.1.call-start = ((), (), s32[]{:S(2)}) async-start(), calls=%async_computation.4 | async-start | bytes 2949120 | tf_op jit(solution)/shard_map/reduce_scatter | solution.py:319
Sparse Core Ops, SparseCore 0:
  333.1 61.9 reduce-scatter.1
